TPU v7x, 32 devices: a whole 2x2x4 slice. The times are simulated.
32 devices in a mesh: dp: 8 (over z, x), seq: 4 (over y, core).
Axes of the slice: x: 2, y: 2, z: 4, core: 2. Of those that a mesh axis runs over, the one named last changes fastest.
Arguments:
- tokens: bfloat16 [16, 1024, 768], P('dp', 'seq'), may hold values from -6 to 6
- early: bfloat16 [16, 1024, 768], P('dp', 'seq'), may hold values from -6 to 6
- cot_backbone: bfloat16 [16, 1024, 768], P('dp', 'seq'), may hold values from -6 to 6
- cot_head: bfloat16 [16, 1024, 768], P('dp', 'seq'), may hold values from -6 to 6
- lengths: int32 [16], P('dp'), may hold values from 1024 to 1024, as said below
- cls_pos: int32 [16], P('dp'), may hold values from 0 to 1023
- back_query: bfloat16 [768, 768], P(('dp', 'seq')), may hold values from -0.3125 to 0.3125
- back_query_bias: bfloat16 [768], P(('dp', 'seq')), may hold values from -3 to 3
- back_key: bfloat16 [768, 768], P(('dp', 'seq')), may hold values from -0.3125 to 0.3125
- back_value: bfloat16 [768, 768], P(('dp', 'seq')), may hold values from -0.21875 to 0.21875
- back_value_bias: bfloat16 [768], P(('dp', 'seq')), may hold values from -3 to 3
- back_output: bfloat16 [768, 768], P(('dp', 'seq')), may hold values from -0.75 to 0.75
- back_output_bias: bfloat16 [768], P(('dp', 'seq')), may hold values from -3 to 3
- back_attn_gain: bfloat16 [768], P(('dp', 'seq')), may hold values from 0.099609375 to 1.8984375
- back_attn_shift: bfloat16 [768], P(('dp', 'seq')), may hold values from -3 to 3
- back_expand: bfloat16 [768, 3072], P(('dp', 'seq')), may hold values from -0.21875 to 0.21875
- back_expand_bias: bfloat16 [3072], P(('dp', 'seq')), may hold values from -3 to 3
- back_reduce: bfloat16 [3072, 768], P(('dp', 'seq')), may hold values from -0.109375 to 0.109375
- back_reduce_bias: bfloat16 [768], P(('dp', 'seq')), may hold values from -3 to 3
- back_ffn_gain: bfloat16 [768], P(('dp', 'seq')), may hold values from 0.099609375 to 1.8984375
- back_ffn_shift: bfloat16 [768], P(('dp', 'seq')), may hold values from -3 to 3
- head_query: bfloat16 [768, 768], P(('dp', 'seq')), may hold values from -0.3125 to 0.3125
- head_query_bias: bfloat16 [768], P(('dp', 'seq')), may hold values from -3 to 3
- head_key: bfloat16 [768, 768], P(('dp', 'seq')), may hold values from -0.3125 to 0.3125
- head_value: bfloat16 [768, 768], P(('dp', 'seq')), may hold values from -0.21875 to 0.21875
- head_value_bias: bfloat16 [768], P(('dp', 'seq')), may hold values from -3 to 3
- head_output: bfloat16 [768, 768], P(('dp', 'seq')), may hold values from -0.75 to 0.75
- head_output_bias: bfloat16 [768], P(('dp', 'seq')), may hold values from -3 to 3
- head_attn_gain: bfloat16 [768], P(('dp', 'seq')), may hold values from 0.099609375 to 1.8984375
- head_attn_shift: bfloat16 [768], P(('dp', 'seq')), may hold values from -3 to 3
- head_expand: bfloat16 [768, 3072], P(('dp', 'seq')), may hold values from -0.21875 to 0.21875
- head_expand_bias: bfloat16 [3072], P(('dp', 'seq')), may hold values from -3 to 3
- head_reduce: bfloat16 [3072, 768], P(('dp', 'seq')), may hold values from -0.109375 to 0.109375
- head_reduce_bias: bfloat16 [768], P(('dp', 'seq')), may hold values from -3 to 3
- head_ffn_gain: bfloat16 [768], P(('dp', 'seq')), may hold values from 0.099609375 to 1.8984375
- head_ffn_shift: bfloat16 [768], P(('dp', 'seq')), may hold values from -3 to 3
Outputs:
- backbone_out: bfloat16 [16, 1024, 768], P('dp', 'seq')
- head_out: bfloat16 [16, 1024, 768], P('dp', 'seq')
- grad_tokens: bfloat16 [16, 1024, 768], P('dp', 'seq')
- grad_early: bfloat16 [16, 1024, 768], P('dp', 'seq')
- grad_back_query: float32 [768, 768], P(('dp', 'seq'))
- grad_back_query_bias: float32 [768], P(('dp', 'seq'))
- grad_back_key: float32 [768, 768], P(('dp', 'seq'))
- grad_back_value: float32 [768, 768], P(('dp', 'seq'))
- grad_back_value_bias: float32 [768], P(('dp', 'seq'))
- grad_back_output: float32 [768, 768], P(('dp', 'seq'))
- grad_back_output_bias: float32 [768], P(('dp', 'seq'))
- grad_back_attn_gain: float32 [768], P(('dp', 'seq'))
- grad_back_attn_shift: float32 [768], P(('dp', 'seq'))
- grad_back_expand: float32 [768, 3072], P(('dp', 'seq'))
- grad_back_expand_bias: float32 [3072], P(('dp', 'seq'))
- grad_back_reduce: float32 [3072, 768], P(('dp', 'seq'))
- grad_back_reduce_bias: float32 [768], P(('dp', 'seq'))
- grad_back_ffn_gain: float32 [768], P(('dp', 'seq'))
- grad_back_ffn_shift: float32 [768], P(('dp', 'seq'))
- grad_head_query: float32 [768, 768], P(('dp', 'seq'))
- grad_head_query_bias: float32 [768], P(('dp', 'seq'))
- grad_head_key: float32 [768, 768], P(('dp', 'seq'))
- grad_head_value: float32 [768, 768], P(('dp', 'seq'))
- grad_head_value_bias: float32 [768], P(('dp', 'seq'))
- grad_head_output: float32 [768, 768], P(('dp', 'seq'))
- grad_head_output_bias: float32 [768], P(('dp', 'seq'))
- grad_head_attn_gain: float32 [768], P(('dp', 'seq'))
- grad_head_attn_shift: float32 [768], P(('dp', 'seq'))
- grad_head_expand: float32 [768, 3072], P(('dp', 'seq'))
- grad_head_expand_bias: float32 [3072], P(('dp', 'seq'))
- grad_head_reduce: float32 [3072, 768], P(('dp', 'seq'))
- grad_head_reduce_bias: float32 [768], P(('dp', 'seq'))
- grad_head_ffn_gain: float32 [768], P(('dp', 'seq'))
- grad_head_ffn_shift: float32 [768], P(('dp', 'seq'))
Inputs may be any that keep to these rules, and one draw needn't show every extreme that they name: `lengths`: the first length positions of a sequence hold tokens, the rest is padding; every sequence has length 1024 (no padding).
All inputs are finite; a program needn't handle non-finite values.
Results may differ from a plain program's by a relative error of at most 0.03.
Values may be sent and summed in bfloat16 or wider, within the bound.
A program may use at most 256 MiB of HBM per device.

v0:
```python
from functools import partial
import math

import jax
import jax.numpy as jnp
from jax import lax
from jax.sharding import PartitionSpec as P

H = 12
HD = 64


EPS = 1e-12
NEG = -1e30


def layer_norm(value, gain, shift):
    mean = jnp.mean(value, axis=-1, keepdims=True)
    centred = value - mean
    spread = jnp.mean(centred * centred, axis=-1, keepdims=True)
    return centred * lax.rsqrt(spread + EPS) * gain + shift


def exact_gelu(value):
    return jax.nn.gelu(value, approximate=False)


def product(left, right):
    return jnp.dot(left, right, preferred_element_type=jnp.float32)


def product_back(left, right):
    return lax.dot_general(
        left, right, (((1,), (1,)), ((), ())), preferred_element_type=jnp.float32
    )


def cross_rows(left, right):
    return lax.dot_general(
        left, right, (((0,), (0,)), ((), ())), preferred_element_type=jnp.float32
    )


def column_sums(value):
    return jnp.sum(value.astype(jnp.float32), axis=0)


def head_scores(queries, keys):
    return jnp.einsum("rhe,khe->hrk", queries, keys, preferred_element_type=jnp.float32) * HD ** (
        -0.5
    )


def forward_fold(queries, length, carry, piece):
    keys_piece, values_piece = piece
    count = keys_piece.shape[0]
    block = math.gcd(count, 512)
    keys_blocks = keys_piece.reshape(count // block, block, H, HD)
    values_blocks = values_piece.reshape(count // block, block, H, HD)

    def forward_step(state, item):
        number, key_block, value_block = item
        first = number * block
        top, total, numer = state
        valid = first + jnp.arange(block, dtype=jnp.int32) < length
        score = jnp.where(valid, head_scores(queries, key_block), NEG)
        new_top = jnp.maximum(top, jnp.max(score, axis=-1))
        weight = jnp.where(valid, jnp.exp(score - new_top[:, :, None]), 0.0)
        decay = jnp.exp(top - new_top)
        total = total * decay + jnp.sum(weight, axis=-1)
        numer = numer * decay[:, :, None] + jnp.einsum(
            "hrk,khe->hre",
            weight.astype(jnp.bfloat16),
            value_block,
            preferred_element_type=jnp.float32,
        )
        return ((new_top, total, numer), None)

    result, _ = lax.scan(
        forward_step,
        carry,
        (jnp.arange(count // block, dtype=jnp.int32), keys_blocks, values_blocks),
    )
    return result


def key_grad_fold(queries, grad_heads, log_total, delta, length, carry, piece, start):
    keys_piece, values_piece = piece
    count = keys_piece.shape[0]
    block = math.gcd(count, 512)
    keys_blocks = keys_piece.reshape(count // block, block, H, HD)
    values_blocks = values_piece.reshape(count // block, block, H, HD)

    def key_step(state, item):
        number, key_block, value_block = item
        first = number * block
        grad_query, grad_keys, grad_values = state
        valid = first + jnp.arange(block, dtype=jnp.int32) < length
        score = jnp.where(valid, head_scores(queries, key_block), NEG)
        chance = jnp.where(valid, jnp.exp(score - log_total[:, :, None]), 0.0)
        grad_chance = jnp.einsum(
            "rhe,khe->hrk", grad_heads, value_block, preferred_element_type=jnp.float32
        )
        grad_score = (chance * (grad_chance - delta[:, :, None])).astype(jnp.bfloat16)
        grad_query = grad_query + jnp.einsum(
            "hrk,khe->rhe", grad_score, key_block, preferred_element_type=jnp.float32
        ) * HD ** (-0.5)
        key_part = (
            jnp.einsum("hrk,rhe->khe", grad_score, queries, preferred_element_type=jnp.float32)
            * HD ** (-0.5)
        ).reshape(block, H * HD)
        value_part = jnp.einsum(
            "hrk,rhe->khe",
            chance.astype(jnp.bfloat16),
            grad_heads,
            preferred_element_type=jnp.float32,
        ).reshape(block, H * HD)
        grad_keys = lax.dynamic_update_slice_in_dim(grad_keys, key_part, first, 0)
        grad_values = lax.dynamic_update_slice_in_dim(grad_values, value_part, first, 0)
        return ((grad_query, grad_keys, grad_values), None)

    result, _ = lax.scan(
        key_step, carry, (jnp.arange(count // block, dtype=jnp.int32), keys_blocks, values_blocks)
    )
    return result


def gather_layer(params):
    return (
        lax.all_gather(params[0], ("dp", "seq"), axis=0, tiled=True),
        lax.all_gather(params[1], ("dp", "seq"), axis=0, tiled=True),
        lax.all_gather(params[2], ("dp", "seq"), axis=0, tiled=True),
        lax.all_gather(params[3], ("dp", "seq"), axis=0, tiled=True),
        lax.all_gather(params[4], ("dp", "seq"), axis=0, tiled=True),
        lax.all_gather(params[5], ("dp", "seq"), axis=0, tiled=True),
        lax.all_gather(params[6], ("dp", "seq"), axis=0, tiled=True),
        lax.all_gather(params[7], ("dp", "seq"), axis=0, tiled=True),
        lax.all_gather(params[8], ("dp", "seq"), axis=0, tiled=True),
        lax.all_gather(params[9], ("dp", "seq"), axis=0, tiled=True),
        lax.all_gather(params[10], ("dp", "seq"), axis=0, tiled=True),
        lax.all_gather(params[11], ("dp", "seq"), axis=0, tiled=True),
        lax.all_gather(params[12], ("dp", "seq"), axis=0, tiled=True),
        lax.all_gather(params[13], ("dp", "seq"), axis=0, tiled=True),
        lax.all_gather(params[14], ("dp", "seq"), axis=0, tiled=True),
    )


def gather_again(params):
    return (
        lax.all_gather(params[0], ("dp", "seq"), axis=0, tiled=True),
        lax.all_gather(params[1], ("dp", "seq"), axis=0, tiled=True),
        lax.all_gather(params[2], ("dp", "seq"), axis=0, tiled=True),
        lax.all_gather(params[3], ("dp", "seq"), axis=0, tiled=True),
        lax.all_gather(params[4], ("dp", "seq"), axis=0, tiled=True),
        lax.all_gather(params[5], ("dp", "seq"), axis=0, tiled=True),
        lax.all_gather(params[6], ("dp", "seq"), axis=0, tiled=True),
        lax.all_gather(params[7], ("dp", "seq"), axis=0, tiled=True),
        lax.all_gather(params[8], ("dp", "seq"), axis=0, tiled=True),
        lax.all_gather(params[9], ("dp", "seq"), axis=0, tiled=True),
        lax.all_gather(params[10], ("dp", "seq"), axis=0, tiled=True),
        lax.all_gather(params[11], ("dp", "seq"), axis=0, tiled=True),
        lax.all_gather(params[12], ("dp", "seq"), axis=0, tiled=True),
        lax.all_gather(params[13], ("dp", "seq"), axis=0, tiled=True),
        lax.all_gather(params[14], ("dp", "seq"), axis=0, tiled=True),
    )


def forward_layer(params, rows_in, length):
    (
        query_w,
        query_bias,
        key_w,
        value_w,
        value_bias,
        output_w,
        output_bias,
        attn_gain,
        attn_shift,
        expand_w,
        expand_bias,
        reduce_w,
        reduce_bias,
        ffn_gain,
        ffn_shift,
    ) = params
    rows = rows_in.shape[0]
    query = (product(rows_in, query_w) + query_bias.astype(jnp.float32)).astype(jnp.bfloat16)
    key = product(rows_in, key_w).astype(jnp.bfloat16)
    value = (product(rows_in, value_w) + value_bias.astype(jnp.float32)).astype(jnp.bfloat16)
    queries = query.reshape(rows, H, HD)
    start_state = (
        jnp.full((H, rows), NEG, jnp.float32),
        jnp.zeros((H, rows), jnp.float32),
        jnp.zeros((H, rows, HD), jnp.float32),
    )
    top, total, numer = forward_fold(
        queries,
        length,
        start_state,
        (
            lax.all_gather(key, "seq", axis=0, tiled=True),
            lax.all_gather(value, "seq", axis=0, tiled=True),
        ),
    )
    attended = jnp.transpose(numer / total[:, :, None], (1, 0, 2)).reshape(rows, H * HD)
    log_total = jnp.transpose(top + jnp.log(total))
    attended_low = attended.astype(jnp.bfloat16)
    summed = (
        rows_in.astype(jnp.float32)
        + product(attended_low, output_w)
        + output_bias.astype(jnp.float32)
    )
    hidden = layer_norm(summed, attn_gain.astype(jnp.float32), attn_shift.astype(jnp.float32))
    hidden_low = hidden.astype(jnp.bfloat16)
    inner = product(hidden_low, expand_w) + expand_bias.astype(jnp.float32)
    active = exact_gelu(inner).astype(jnp.bfloat16)
    pre_final = hidden + product(active, reduce_w) + reduce_bias.astype(jnp.float32)
    result = layer_norm(pre_final, ffn_gain.astype(jnp.float32), ffn_shift.astype(jnp.float32))
    saved = (
        rows_in,
        query,
        key,
        value,
        attended,
        attended_low,
        log_total,
        summed,
        hidden,
        hidden_low,
        inner,
        active,
        pre_final,
    )
    return (result, saved)


def backward_layer(params, saved, grad_out, length):
    (
        query_w,
        query_bias,
        key_w,
        value_w,
        value_bias,
        output_w,
        output_bias,
        attn_gain,
        attn_shift,
        expand_w,
        expand_bias,
        reduce_w,
        reduce_bias,
        ffn_gain,
        ffn_shift,
    ) = params
    (
        rows_in,
        query,
        key,
        value,
        attended,
        attended_low,
        log_total,
        summed,
        hidden,
        hidden_low,
        inner,
        active,
        pre_final,
    ) = saved
    rows = rows_in.shape[0]
    _, norm_second = jax.vjp(
        layer_norm, pre_final, ffn_gain.astype(jnp.float32), ffn_shift.astype(jnp.float32)
    )
    grad_pre, grad_ffn_gain, grad_ffn_shift = norm_second(grad_out)
    grad_outer = grad_pre.astype(jnp.bfloat16)
    grad_reduce = cross_rows(active, grad_outer)
    grad_reduce_bias = column_sums(grad_outer)
    grad_active = product_back(grad_outer, reduce_w)
    _, gelu_back = jax.vjp(exact_gelu, inner)
    grad_inner = gelu_back(grad_active)[0].astype(jnp.bfloat16)
    grad_expand = cross_rows(hidden_low, grad_inner)
    grad_expand_bias = column_sums(grad_inner)
    grad_hidden = grad_pre + product_back(grad_inner, expand_w)
    _, norm_first = jax.vjp(
        layer_norm, summed, attn_gain.astype(jnp.float32), attn_shift.astype(jnp.float32)
    )
    grad_summed, grad_attn_gain, grad_attn_shift = norm_first(grad_hidden)
    grad_branch = grad_summed.astype(jnp.bfloat16)
    grad_output = cross_rows(attended_low, grad_branch)
    grad_output_bias = column_sums(grad_branch)
    grad_attended = product_back(grad_branch, output_w).astype(jnp.bfloat16)
    grad_heads = grad_attended.reshape(rows, H, HD)
    delta = jnp.sum(grad_heads.astype(jnp.float32) * attended.reshape(rows, H, HD), axis=-1)
    queries = query.reshape(rows, H, HD)
    full_rows = rows * lax.axis_size("seq")
    start_state = (
        jnp.zeros((rows, H, HD), jnp.float32),
        jnp.zeros((full_rows, H * HD), jnp.float32),
        jnp.zeros((full_rows, H * HD), jnp.float32),
    )
    folder = partial(
        key_grad_fold, queries, grad_heads, jnp.transpose(log_total), jnp.transpose(delta), length
    )
    grad_query_heads, grad_keys_all, grad_values_all = folder(
        start_state,
        (
            lax.all_gather(key, "seq", axis=0, tiled=True),
            lax.all_gather(value, "seq", axis=0, tiled=True),
        ),
        jnp.int32(0),
    )
    grad_query = grad_query_heads.reshape(rows, H * HD)
    grad_key, grad_value = (
        lax.psum_scatter(
            grad_keys_all.astype(jnp.bfloat16), "seq", scatter_dimension=0, tiled=True
        ).astype(jnp.float32),
        lax.psum_scatter(
            grad_values_all.astype(jnp.bfloat16), "seq", scatter_dimension=0, tiled=True
        ).astype(jnp.float32),
    )
    grad_query_low = grad_query.astype(jnp.bfloat16)
    grad_key_low = grad_key.astype(jnp.bfloat16)
    grad_value_low = grad_value.astype(jnp.bfloat16)
    grad_query_w = cross_rows(rows_in, grad_query_low)
    grad_query_bias = column_sums(grad_query_low)
    grad_key_w = cross_rows(rows_in, grad_key_low)
    grad_value_w = cross_rows(rows_in, grad_value_low)
    grad_value_bias = column_sums(grad_value_low)
    grad_in = (
        grad_summed
        + product_back(grad_query_low, query_w)
        + product_back(grad_key_low, key_w)
        + product_back(grad_value_low, value_w)
    )
    grads = (
        grad_query_w,
        grad_query_bias,
        grad_key_w,
        grad_value_w,
        grad_value_bias,
        grad_output,
        grad_output_bias,
        grad_attn_gain,
        grad_attn_shift,
        grad_expand,
        grad_expand_bias,
        grad_reduce,
        grad_reduce_bias,
        grad_ffn_gain,
        grad_ffn_shift,
    )
    return (grad_in, grads)


def on_device(
    tokens,
    early,
    cot_backbone,
    cot_head,
    lengths,
    cls_pos,
    back_query,
    back_query_bias,
    back_key,
    back_value,
    back_value_bias,
    back_output,
    back_output_bias,
    back_attn_gain,
    back_attn_shift,
    back_expand,
    back_expand_bias,
    back_reduce,
    back_reduce_bias,
    back_ffn_gain,
    back_ffn_shift,
    head_query,
    head_query_bias,
    head_key,
    head_value,
    head_value_bias,
    head_output,
    head_output_bias,
    head_attn_gain,
    head_attn_shift,
    head_expand,
    head_expand_bias,
    head_reduce,
    head_reduce_bias,
    head_ffn_gain,
    head_ffn_shift,
):
    shards = (
        (
            back_query,
            back_query_bias,
            back_key,
            back_value,
            back_value_bias,
            back_output,
            back_output_bias,
            back_attn_gain,
            back_attn_shift,
            back_expand,
            back_expand_bias,
            back_reduce,
            back_reduce_bias,
            back_ffn_gain,
            back_ffn_shift,
        ),
        (
            head_query,
            head_query_bias,
            head_key,
            head_value,
            head_value_bias,
            head_output,
            head_output_bias,
            head_attn_gain,
            head_attn_shift,
            head_expand,
            head_expand_bias,
            head_reduce,
            head_reduce_bias,
            head_ffn_gain,
            head_ffn_shift,
        ),
    )
    rows = tokens.shape[1]
    offset = lax.axis_index("seq") * rows
    positions = offset + jnp.arange(rows, dtype=jnp.int32)
    backbone_rows = []
    head_rows = []
    stored = []
    gathered_sets = []
    for number in range(tokens.shape[0]):
        forward_params = [gather_layer(layer_shards) for layer_shards in shards]
        length = lengths[number]
        backbone, back_saved = forward_layer(forward_params[0], tokens[number], length)
        backbone_low = backbone.astype(jnp.bfloat16)
        is_cls = (positions == cls_pos[number])[:, None]
        head_in = jnp.where(is_cls, backbone_low, early[number])
        head_result, head_saved = forward_layer(forward_params[1], head_in, length)
        backbone_rows.append(backbone_low)
        head_rows.append(head_result.astype(jnp.bfloat16))
        stored.append((back_saved, head_saved))
        gathered_sets.append(forward_params)
    back_sums = [jnp.zeros(weight_full.shape, jnp.float32) for weight_full in gathered_sets[0][0]]
    head_sums = [jnp.zeros(weight_full.shape, jnp.float32) for weight_full in gathered_sets[0][1]]
    grad_token_rows = []
    grad_early_rows = []
    for number in range(tokens.shape[0]):
        backward_params = [gather_again(layer_shards) for layer_shards in shards]
        length = lengths[number]
        valid_rows = (positions < length)[:, None]
        is_cls = (positions == cls_pos[number])[:, None]
        grad_head_out = jnp.where(valid_rows, cot_head[number].astype(jnp.float32), 0.0)
        grad_head_in, head_grads = backward_layer(
            backward_params[1], stored[number][1], grad_head_out, length
        )
        grad_early_rows.append(jnp.where(is_cls, 0.0, grad_head_in).astype(jnp.bfloat16))
        grad_backbone = jnp.where(
            valid_rows, cot_backbone[number].astype(jnp.float32), 0.0
        ) + jnp.where(is_cls, grad_head_in, 0.0)
        grad_in, back_grads = backward_layer(
            backward_params[0], stored[number][0], grad_backbone, length
        )
        grad_token_rows.append(grad_in.astype(jnp.bfloat16))
        back_sums = [running + term for running, term in zip(back_sums, back_grads)]
        head_sums = [running + term for running, term in zip(head_sums, head_grads)]
    combined = back_sums + head_sums
    shared = (
        lax.psum_scatter(combined[0], ("dp", "seq"), scatter_dimension=0, tiled=True),
        lax.psum_scatter(combined[1], ("dp", "seq"), scatter_dimension=0, tiled=True),
        lax.psum_scatter(combined[2], ("dp", "seq"), scatter_dimension=0, tiled=True),
        lax.psum_scatter(combined[3], ("dp", "seq"), scatter_dimension=0, tiled=True),
        lax.psum_scatter(combined[4], ("dp", "seq"), scatter_dimension=0, tiled=True),
        lax.psum_scatter(combined[5], ("dp", "seq"), scatter_dimension=0, tiled=True),
        lax.psum_scatter(combined[6], ("dp", "seq"), scatter_dimension=0, tiled=True),
        lax.psum_scatter(combined[7], ("dp", "seq"), scatter_dimension=0, tiled=True),
        lax.psum_scatter(combined[8], ("dp", "seq"), scatter_dimension=0, tiled=True),
        lax.psum_scatter(combined[9], ("dp", "seq"), scatter_dimension=0, tiled=True),
        lax.psum_scatter(combined[10], ("dp", "seq"), scatter_dimension=0, tiled=True),
        lax.psum_scatter(combined[11], ("dp", "seq"), scatter_dimension=0, tiled=True),
        lax.psum_scatter(combined[12], ("dp", "seq"), scatter_dimension=0, tiled=True),
        lax.psum_scatter(combined[13], ("dp", "seq"), scatter_dimension=0, tiled=True),
        lax.psum_scatter(combined[14], ("dp", "seq"), scatter_dimension=0, tiled=True),
        lax.psum_scatter(combined[15], ("dp", "seq"), scatter_dimension=0, tiled=True),
        lax.psum_scatter(combined[16], ("dp", "seq"), scatter_dimension=0, tiled=True),
        lax.psum_scatter(combined[17], ("dp", "seq"), scatter_dimension=0, tiled=True),
        lax.psum_scatter(combined[18], ("dp", "seq"), scatter_dimension=0, tiled=True),
        lax.psum_scatter(combined[19], ("dp", "seq"), scatter_dimension=0, tiled=True),
        lax.psum_scatter(combined[20], ("dp", "seq"), scatter_dimension=0, tiled=True),
        lax.psum_scatter(combined[21], ("dp", "seq"), scatter_dimension=0, tiled=True),
        lax.psum_scatter(combined[22], ("dp", "seq"), scatter_dimension=0, tiled=True),
        lax.psum_scatter(combined[23], ("dp", "seq"), scatter_dimension=0, tiled=True),
        lax.psum_scatter(combined[24], ("dp", "seq"), scatter_dimension=0, tiled=True),
        lax.psum_scatter(combined[25], ("dp", "seq"), scatter_dimension=0, tiled=True),
        lax.psum_scatter(combined[26], ("dp", "seq"), scatter_dimension=0, tiled=True),
        lax.psum_scatter(combined[27], ("dp", "seq"), scatter_dimension=0, tiled=True),
        lax.psum_scatter(combined[28], ("dp", "seq"), scatter_dimension=0, tiled=True),
        lax.psum_scatter(combined[29], ("dp", "seq"), scatter_dimension=0, tiled=True),
    )
    return (
        jnp.stack(backbone_rows),
        jnp.stack(head_rows),
        jnp.stack(grad_token_rows),
        jnp.stack(grad_early_rows),
    ) + tuple(shared)


def solution(mesh):
    placed = (
        P("dp", "seq", None),
        P("dp", "seq", None),
        P("dp", "seq", None),
        P("dp", "seq", None),
        P("dp"),
        P("dp"),
        P(("dp", "seq"), None),
        P(("dp", "seq")),
        P(("dp", "seq"), None),
        P(("dp", "seq"), None),
        P(("dp", "seq")),
        P(("dp", "seq"), None),
        P(("dp", "seq")),
        P(("dp", "seq")),
        P(("dp", "seq")),
        P(("dp", "seq"), None),
        P(("dp", "seq")),
        P(("dp", "seq"), None),
        P(("dp", "seq")),
        P(("dp", "seq")),
        P(("dp", "seq")),
        P(("dp", "seq"), None),
        P(("dp", "seq")),
        P(("dp", "seq"), None),
        P(("dp", "seq"), None),
        P(("dp", "seq")),
        P(("dp", "seq"), None),
        P(("dp", "seq")),
        P(("dp", "seq")),
        P(("dp", "seq")),
        P(("dp", "seq"), None),
        P(("dp", "seq")),
        P(("dp", "seq"), None),
        P(("dp", "seq")),
        P(("dp", "seq")),
        P(("dp", "seq")),
    )
    return jax.shard_map(
        on_device,
        mesh=mesh,
        in_specs=placed,
        out_specs=(
            P("dp", "seq", None),
            P("dp", "seq", None),
            P("dp", "seq", None),
            P("dp", "seq", None),
            P(("dp", "seq"), None),
            P(("dp", "seq")),
            P(("dp", "seq"), None),
            P(("dp", "seq"), None),
            P(("dp", "seq")),
            P(("dp", "seq"), None),
            P(("dp", "seq")),
            P(("dp", "seq")),
            P(("dp", "seq")),
            P(("dp", "seq"), None),
            P(("dp", "seq")),
            P(("dp", "seq"), None),
            P(("dp", "seq")),
            P(("dp", "seq")),
            P(("dp", "seq")),
            P(("dp", "seq"), None),
            P(("dp", "seq")),
            P(("dp", "seq"), None),
            P(("dp", "seq"), None),
            P(("dp", "seq")),
            P(("dp", "seq"), None),
            P(("dp", "seq")),
            P(("dp", "seq")),
            P(("dp", "seq")),
            P(("dp", "seq"), None),
            P(("dp", "seq")),
            P(("dp", "seq"), None),
            P(("dp", "seq")),
            P(("dp", "seq")),
            P(("dp", "seq")),
        ),
        check_vma=False,
    )
```

profile of v0, /device:TPU:0, one launch (start us, length us, event | category | flops | bytes accessed | tf_op | source)
XLA Modules:
  0.0 2860.4 jit_solution(13735710670536920322)
XLA Ops:
  9.5 58.2 %all-gather.21.cloned.1.call-done = bf16[768,768]{1,0:T(8,128)(2,1)} async-done(((bf16[24,768]{1,0:T(8,128)(2,1)}), bf16[768,768]{1,0:T(8,128)(2,1)}) %all-gather.21.cloned.1.call-update) | async-done | bytes 1179664 | tf_op jit(solution)/shard_map/all_gather | solution.py:132
  85.6 40.9 %all-reduce.37 = (bf16[768]{0:T(1024)(128)(2,1)S(1)}, bf16[768]{0:T(1024)(128)(2,1)S(1)}, bf16[3072]{0:T(1024)(128)(2,1)S(1)}, bf16[768]{0:T(1024)(128)(2,1)S(1)...) all-reduce(bf16[768]{0:T(1024)(128)(2,1)S(1)} %dynamic-update-slice, ...), channel_id=1, replica_groups=mesh['dp'=8,'seq'=4] {'dp','seq'}, use_global_device_ids=true, to_apply=%add.8 | all-reduce | flops 18432 | bytes 73728
  411.1 39.9 %all-gather.35.cloned.1.call-done = bf16[3072,768]{1,0:T(8,128)(2,1)} async-done(((bf16[96,768]{1,0:T(8,128)(2,1)}), bf16[3072,768]{1,0:T(8,128)(2,1)}) %all-gather.35.cloned.1.call-update) | async-done | bytes 4718608 | tf_op jit(solution)/shard_map/all_gather | solution.py:141
  458.8 47.5 %all-gather.41.cloned.1.call-done = bf16[768,768]{1,0:T(8,128)(2,1)} async-done(((bf16[24,768]{1,0:T(8,128)(2,1)}), bf16[768,768]{1,0:T(8,128)(2,1)}) %all-gather.41.cloned.1.call-update) | async-done | bytes 1179664 | tf_op jit(solution)/shard_map/all_gather | solution.py:132
  509.0 53.0 %all-gather.47.cloned.1.call-done = bf16[768,768]{1,0:T(8,128)(2,1)} async-done(((bf16[24,768]{1,0:T(8,128)(2,1)}), bf16[768,768]{1,0:T(8,128)(2,1)}) %all-gather.47.cloned.1.call-update) | async-done | bytes 1179664 | tf_op jit(solution)/shard_map/all_gather | solution.py:133
  575.3 42.5 %all-gather.45.cloned.1.call-done = bf16[768,768]{1,0:T(8,128)(2,1)} async-done(((bf16[24,768]{1,0:T(8,128)(2,1)}), bf16[768,768]{1,0:T(8,128)(2,1)}) %all-gather.45.cloned.1.call-update) | async-done | bytes 1179664 | tf_op jit(solution)/shard_map/all_gather | solution.py:130
  714.5 43.3 %all-gather.51.cloned.1.call-done = bf16[768,768]{1,0:T(8,128)(2,1)} async-done(((bf16[24,768]{1,0:T(8,128)(2,1)}), bf16[768,768]{1,0:T(8,128)(2,1)}) %all-gather.51.cloned.1.call-update) | async-done | bytes 1179664 | tf_op jit(solution)/shard_map/all_gather | solution.py:135
  835.5 52.4 %all-gather.55.cloned.1.call-done = bf16[3072,768]{1,0:T(8,128)(2,1)} async-done(((bf16[96,768]{1,0:T(8,128)(2,1)}), bf16[3072,768]{1,0:T(8,128)(2,1)}) %all-gather.55.cloned.1.call-update) | async-done | bytes 4718608 | tf_op jit(solution)/shard_map/all_gather | solution.py:141
  929.7 39.2 %while.126 = (s32[]{:T(128)}, f32[256,12,64]{0,2,1:T(8,128)}, bf16[1024,768]{0,1:T(8,128)(2,1)}, bf16[1024,768]{0,1:T(8,128)(2,1)}, bf16[2,512,12,64]{1,3,2,0:T(...) while((s32[]{:T(128)}, f32[256,12,64]{0,2,1:T(8,128)}, ...), condition=%wide.region_56.57_spmd.clone, body=%wide.region_55.56_spmd.clone.sunk | while | flops 1026884608 | bytes 114182432 | solution.py:122
  978.0 41.2 %while.124 = (s32[]{:T(128)}, f32[256,12,64]{0,2,1:T(8,128)}, bf16[1024,768]{0,1:T(8,128)(2,1)}, bf16[1024,768]{0,1:T(8,128)(2,1)}, bf16[2,512,12,64]{1,3,2,0:T(...) while((s32[]{:T(128)}, f32[256,12,64]{0,2,1:T(8,128)}, ...), condition=%wide.region_38.39_spmd.clone, body=%wide.region_37.38_spmd.clone.sunk | while | flops 1026884608 | bytes 101599456 | solution.py:122
  1120.5 41.0 %while.125 = (s32[]{:T(128)}, f32[256,12,64]{0,2,1:T(8,128)}, bf16[1024,768]{0,1:T(8,128)(2,1)}, bf16[1024,768]{0,1:T(8,128)(2,1)}, bf16[2,512,12,64]{1,3,2,0:T(...) while((s32[]{:T(128)}, f32[256,12,64]{0,2,1:T(8,128)}, ...), condition=%wide.region_47.48_spmd.clone, body=%wide.region_46.47_spmd.clone.sunk | while | flops 1026884608 | bytes 101599456 | solution.py:122
  1351.6 97.1 %all-reduce.40.cloned.1.call-done = (f32[768]{0:T(1024)}, f32[768]{0:T(1024)}, f32[768]{0:T(1024)}, f32[768]{0:T(1024)}, f32[768]{0:T(1024)}, /*index=5*/f32[307...) async-done(((f32[768]{0:T(1024)}, f32[768]{0:T(1024)}, ...) | async-done | bytes 73744
  1471.4 84.5 %reduce-scatter.49.cloned.1.call-done = f32[24,768]{1,0:T(8,128)} async-done(((f32[768,768]{1,0:T(8,128)}), f32[24,768]{1,0:T(8,128)}) %reduce-scatter.49.cloned.1.call-update) | async-done | bytes 73744 | tf_op jit(solution)/shard_map/reduce_scatter | solution.py:488
  1555.9 104.5 %reduce-scatter.55.cloned.1.call-done = f32[24,768]{1,0:T(8,128)} async-done(((f32[768,768]{1,0:T(8,128)}), f32[24,768]{1,0:T(8,128)}) %reduce-scatter.55.cloned.1.call-update) | async-done | bytes 73744 | tf_op jit(solution)/shard_map/reduce_scatter | solution.py:493
  1660.4 104.5 %reduce-scatter.61.cloned.1.call-done = f32[24,768]{1,0:T(8,128)} async-done(((f32[768,768]{1,0:T(8,128)}), f32[24,768]{1,0:T(8,128)}) %reduce-scatter.61.cloned.1.call-update) | async-done | bytes 73744
  1764.9 104.3 %reduce-scatter.43.cloned.1.call-done = f32[24,768]{1,0:T(8,128)} async-done(((f32[768,768]{1,0:T(8,128)}), f32[24,768]{1,0:T(8,128)}) %reduce-scatter.43.cloned.1.call-update) | async-done | bytes 73744 | tf_op jit(solution)/shard_map/reduce_scatter | solution.py:478
  1869.2 104.6 %reduce-scatter.51.cloned.1.call-done = f32[24,768]{1,0:T(8,128)} async-done(((f32[768,768]{1,0:T(8,128)}), f32[24,768]{1,0:T(8,128)}) %reduce-scatter.51.cloned.1.call-update) | async-done | bytes 73744 | tf_op jit(solution)/shard_map/reduce_scatter | solution.py:490
  1973.8 104.5 %reduce-scatter.53.cloned.1.call-done = f32[24,768]{1,0:T(8,128)} async-done(((f32[768,768]{1,0:T(8,128)}), f32[24,768]{1,0:T(8,128)}) %reduce-scatter.53.cloned.1.call-update) | async-done | bytes 73744 | tf_op jit(solution)/shard_map/reduce_scatter | solution.py:491
  2078.3 104.3 %reduce-scatter.63.cloned.1.call-done = f32[24,768]{1,0:T(8,128)} async-done(((f32[768,768]{1,0:T(8,128)}), f32[24,768]{1,0:T(8,128)}) %reduce-scatter.63.cloned.1.call-update) | async-done | bytes 73744
  2182.6 104.3 %reduce-scatter.65.cloned.1.call-done = f32[24,768]{1,0:T(8,128)} async-done(((f32[768,768]{1,0:T(8,128)}), f32[24,768]{1,0:T(8,128)}) %reduce-scatter.65.cloned.1.call-update) | async-done | bytes 73744
  2286.9 141.7 %reduce-scatter.57.cloned.1.call-done = f32[24,3072]{1,0:T(8,128)} async-done(((f32[768,3072]{1,0:T(8,128)}), f32[24,3072]{1,0:T(8,128)}) %reduce-scatter.57.cloned.1.call-update) | async-done | bytes 294928 | tf_op jit(solution)/shard_map/reduce_scatter | solution.py:497
  2428.7 141.5 %reduce-scatter.59.cloned.1.call-done = f32[96,768]{1,0:T(8,128)} async-done(((f32[3072,768]{1,0:T(8,128)}), f32[96,768]{1,0:T(8,128)}) %reduce-scatter.59.cloned.1.call-update) | async-done | bytes 294928 | tf_op jit(solution)/shard_map/reduce_scatter | solution.py:499
  2570.2 141.7 %reduce-scatter.45.cloned.1.call-done = f32[24,3072]{1,0:T(8,128)} async-done(((f32[768,3072]{1,0:T(8,128)}), f32[24,3072]{1,0:T(8,128)}) %reduce-scatter.45.cloned.1.call-update) | async-done | bytes 294928 | tf_op jit(solution)/shard_map/reduce_scatter | solution.py:482
  2711.8 141.6 %reduce-scatter.47.cloned.1.call-done = f32[96,768]{1,0:T(8,128)} async-done(((f32[3072,768]{1,0:T(8,128)}), f32[96,768]{1,0:T(8,128)}) %reduce-scatter.47.cloned.1.call-update) | async-done | bytes 294928 | tf_op jit(solution)/shard_map/reduce_scatter | solution.py:484
  (1367 shorter events, 1130.4 us)
Async XLA Ops:
  9.4 190.6 %all-gather.23.cloned.1.call-start = ((), (), s32[]{:S(2)}) async-start(), calls=%async_computation.21 | async-start | bytes 1966080 | tf_op jit(solution)/shard_map/all_gather | solution.py:201
  132.5 253.8 %all-gather.33.cloned.1.call-start = ((), (), s32[]{:S(2)}) async-start(), calls=%async_computation.26 | async-start | bytes 4866048 | tf_op jit(solution)/shard_map/all_gather | solution.py:139
  133.2 317.8 %all-gather.35.cloned.1.call-start = ((), (), s32[]{:S(2)}) async-start(), calls=%async_computation.27 | async-start | bytes 4866048 | tf_op jit(solution)/shard_map/all_gather | solution.py:141
  133.8 372.5 %all-gather.41.cloned.1.call-start = ((), (), s32[]{:S(2)}) async-start(), calls=%async_computation.30 | async-start | bytes 1216512 | tf_op jit(solution)/shard_map/all_gather | solution.py:132
  134.5 427.4 %all-gather.47.cloned.1.call-start = ((), (), s32[]{:S(2)}) async-start(), calls=%async_computation.33 | async-start | bytes 1216512 | tf_op jit(solution)/shard_map/all_gather | solution.py:133
  135.1 482.7 %all-gather.45.cloned.1.call-start = ((), (), s32[]{:S(2)}) async-start(), calls=%async_computation.32 | async-start | bytes 1216512 | tf_op jit(solution)/shard_map/all_gather | solution.py:130
  135.9 501.9 %all-gather.43.cloned.1.call-start = ((), (), s32[]{:S(2)}) async-start(), calls=%async_computation.31 | async-start | bytes 1966080 | tf_op jit(solution)/shard_map/all_gather | solution.py:201
  567.9 255.3 %all-gather.53.cloned.1.call-start = ((), (), s32[]{:S(2)}) async-start(), calls=%async_computation.36 | async-start | bytes 4866048 | tf_op jit(solution)/shard_map/all_gather | solution.py:139
  568.6 319.3 %all-gather.55.cloned.1.call-start = ((), (), s32[]{:S(2)}) async-start(), calls=%async_computation.37 | async-start | bytes 4866048 | tf_op jit(solution)/shard_map/all_gather | solution.py:141
  569.2 458.4 %reduce-scatter.35.cloned.1.call-start = ((), (), s32[]{:S(2)}) async-start(), calls=%async_computation.44 | async-start | bytes 1966080 | tf_op jit(solution)/shard_map/reduce_scatter | solution.py:314
  1019.9 203.1 %reduce-scatter.33.cloned.1.call-start = ((), (), s32[]{:S(2)}) async-start(), calls=%async_computation.43 | async-start | bytes 1966080 | tf_op jit(solution)/shard_map/reduce_scatter | solution.py:317
  1204.7 244.0 %all-reduce.40.cloned.1.call-start = ((), (), s32[]{:S(2)}) async-start(), calls=%async_computation.60 | async-start | bytes 180224
  1233.3 322.6 %reduce-scatter.49.cloned.1.call-start = ((), (), s32[]{:S(2)}) async-start(), calls=%async_computation.51 | async-start | bytes 2433024 | tf_op jit(solution)/shard_map/reduce_scatter | solution.py:488
  1237.1 423.3 %reduce-scatter.55.cloned.1.call-start = ((), (), s32[]{:S(2)}) async-start(), calls=%async_computation.54 | async-start | bytes 2433024 | tf_op jit(solution)/shard_map/reduce_scatter | solution.py:493
  1240.1 524.8 %reduce-scatter.61.cloned.1.call-start = ((), (), s32[]{:S(2)}) async-start(), calls=%async_computation.57 | async-start | bytes 2433024
  1246.1 623.1 %reduce-scatter.43.cloned.1.call-start = ((), (), s32[]{:S(2)}) async-start(), calls=%async_computation.48 | async-start | bytes 2433024 | tf_op jit(solution)/shard_map/reduce_scatter | solution.py:478
  1249.1 724.7 %reduce-scatter.51.cloned.1.call-start = ((), (), s32[]{:S(2)}) async-start(), calls=%async_computation.52 | async-start | bytes 2433024 | tf_op jit(solution)/shard_map/reduce_scatter | solution.py:490
  1252.1 826.2 %reduce-scatter.53.cloned.1.call-start = ((), (), s32[]{:S(2)}) async-start(), calls=%async_computation.53 | async-start | bytes 2433024 | tf_op jit(solution)/shard_map/reduce_scatter | solution.py:491
  1255.0 927.6 %reduce-scatter.63.cloned.1.call-start = ((), (), s32[]{:S(2)}) async-start(), calls=%async_computation.58 | async-start | bytes 2433024
  1298.5 988.4 %reduce-scatter.65.cloned.1.call-start = ((), (), s32[]{:S(2)}) async-start(), calls=%async_computation.59 | async-start | bytes 2433024
  1304.6 1124.0 %reduce-scatter.57.cloned.1.call-start = ((), (), s32[]{:S(2)}) async-start(), calls=%async_computation.55 | async-start | bytes 9732096 | tf_op jit(solution)/shard_map/reduce_scatter | solution.py:497
  1313.4 1256.8 %reduce-scatter.59.cloned.1.call-start = ((), (), s32[]{:S(2)}) async-start(), calls=%async_computation.56 | async-start | bytes 9732096 | tf_op jit(solution)/shard_map/reduce_scatter | solution.py:499
  1322.4 1389.4 %reduce-scatter.45.cloned.1.call-start = ((), (), s32[]{:S(2)}) async-start(), calls=%async_computation.49 | async-start | bytes 9732096 | tf_op jit(solution)/shard_map/reduce_scatter | solution.py:482
  1331.9 1521.5 %reduce-scatter.47.cloned.1.call-start = ((), (), s32[]{:S(2)}) async-start(), calls=%async_computation.50 | async-start | bytes 9732096 | tf_op jit(solution)/shard_map/reduce_scatter | solution.py:484
  (424 other events, 7460.5 us)
Sparse Core Ops, SparseCore 0:
  10.9 56.6 all-gather.20
  70.6 52.9 all-gather.26
  126.5 52.9 all-gather.24
  224.4 53.9 all-gather.30
  322.7 63.5 all-gather.32
  389.1 61.9 all-gather.34
  509.0 52.8 all-gather.46
  564.9 52.8 all-gather.44
  703.8 53.9 all-gather.50
  760.7 62.4 all-gather.52
  825.9 61.9 all-gather.54
  1298.9 149.7 all-reduce.39
  1454.4 101.4 reduce-scatter.48
  1561.8 98.6 reduce-scatter.54
  1666.3 98.5 reduce-scatter.60
  1770.6 98.5 reduce-scatter.42
  1875.1 98.6 reduce-scatter.50
  1979.7 98.5 reduce-scatter.52
  2084.0 98.5 reduce-scatter.62
  2188.3 98.5 reduce-scatter.64
  2293.4 135.2 reduce-scatter.56
  2435.0 135.1 reduce-scatter.58
  2576.6 135.1 reduce-scatter.44
  2718.3 135.0 reduce-scatter.46
  (17 shorter events, 427.7 us)
where the time goes:
time: 2870 us; the launch traced here: 2860 us
  waiting for transfers between devices  2120 us (74%)
  matrix products  369 us (13%)
  local copies, waits for them, and re-layouts  189 us (7%)
  other arithmetic  112 us (4%)
  blocking collectives  40.9 us (1%)
    unnamed x45, waiting for transfers between devices  420 us
    reduce_scatter x1, waiting for transfers between devices, on_device(): lax.psum_scatter(combined[24], ('dp', 'seq'), scatter_dimension=0, tiled=...  142 us
    reduce_scatter x1, waiting for transfers between devices, on_device(): lax.psum_scatter(combined[9], ('dp', 'seq'), scatter_dimension=0, tiled=T...  142 us
    reduce_scatter x1, waiting for transfers between devices, on_device(): lax.psum_scatter(combined[11], ('dp', 'seq'), scatter_dimension=0, tiled=...  142 us
    reduce_scatter x1, waiting for transfers between devices, on_device(): lax.psum_scatter(combined[26], ('dp', 'seq'), scatter_dimension=0, tiled=...  141 us
    all_gather x2, waiting for transfers between devices, gather_layer(): lax.all_gather(params[2], ('dp', 'seq'), axis=0, tiled=True)  106 us
    reduce_scatter x1, waiting for transfers between devices, on_device(): lax.psum_scatter(combined[17], ('dp', 'seq'), scatter_dimension=0, tiled=...  105 us
    reduce_scatter x1, waiting for transfers between devices, on_device(): lax.psum_scatter(combined[20], ('dp', 'seq'), scatter_dimension=0, tiled=...  105 us
  transfers between devices with their start and end apart: 41, of which 35 were waited for; matrix products, arithmetic and copies ran while one was open for 17% of the time, Pallas kernels for 0%

commit v1 on v0

v1 whole, which is shorter than its diff:
```python
from functools import partial
import math

import jax
import jax.numpy as jnp
from jax import lax
from jax.experimental import pallas as pl
from jax.experimental.pallas import tpu as pltpu
from jax.sharding import PartitionSpec as P

H = 12
HD = 64
EPS = 1e-12
NEG = -1e30
MIN_LEN = 1024
BF = jnp.bfloat16
F32 = jnp.float32
MESH = pl.DeviceIdType.MESH
VMEM_LIMIT = 60 * 1024 * 1024


def mm(left, right):
    return lax.dot_general(left, right, (((1,), (0,)), ((), ())), preferred_element_type=F32)


def mm_nt(left, right):
    return lax.dot_general(left, right, (((1,), (1,)), ((), ())), preferred_element_type=F32)


def mm_tn(left, right):
    return lax.dot_general(left, right, (((0,), (0,)), ((), ())), preferred_element_type=F32)


def whole(shape):
    return pl.BlockSpec(shape, lambda *_: (0,) * len(shape))


def params_of(semantics):
    return pltpu.CompilerParams(dimension_semantics=semantics, vmem_limit_bytes=VMEM_LIMIT)


def qkv_kernel(x_ref, w_ref, p_ref, q_ref, kv_ref):
    j = pl.program_id(0)
    out = mm(x_ref[...], w_ref[0])

    @pl.when(j == 0)
    def _():
        q_ref[...] = (out + p_ref[0:1, :]).astype(BF)

    @pl.when(j == 1)
    def _():
        kv_ref[0] = out.astype(BF)

    @pl.when(j == 2)
    def _():
        kv_ref[0] = (out + p_ref[1:2, :]).astype(BF)


def qkv(x, w4, params):
    n, d = x.shape
    return pl.pallas_call(
        qkv_kernel,
        name="qkv",
        grid=(3,),
        in_specs=[
            whole((n, d)),
            pl.BlockSpec((1, d, d), lambda j: (j, 0, 0)),
            whole(params.shape),
        ],
        out_specs=[
            whole((n, d)),
            pl.BlockSpec((1, n, d), lambda j: (jnp.maximum(j - 1, 0), 0, 0)),
        ],
        out_shape=[
            jax.ShapeDtypeStruct((n, d), BF),
            jax.ShapeDtypeStruct((2, n, d), BF),
        ],
        compiler_params=params_of(("arbitrary",)),
        cost_estimate=pl.CostEstimate(flops=6 * n * d * d, bytes_accessed=6 * d * d + 8 * n * d, transcendentals=0),
    )(x, w4, params)


def half_masks(n):
    lane = lax.broadcasted_iota(jnp.int32, (n, 2 * HD), 1)
    return lane < HD


def attend_kernel(pieces, masked, chunk, *refs):
    q_ref = refs[0]
    kv_refs = refs[1 : 1 + pieces]
    refs = refs[1 + pieces :]
    bias_ref = None
    if masked:
        bias_ref, refs = refs[0], refs[1:]
    att_ref, lse_ref = refs
    n = q_ref.shape[0]
    for start in range(0, n, chunk):
        rows = pl.ds(start, chunk)
        low = half_masks(chunk)
        q = q_ref[rows, :] * jnp.asarray(HD**-0.5, BF)
        outs = []
        logs = []
        for side in range(2):
            qm = jnp.where(low if side == 0 else ~low, q, jnp.zeros_like(q))
            scores = []
            for t in range(pieces):
                s = mm_nt(qm, kv_refs[t][0])
                if masked:
                    s = s + bias_ref[t]
                scores.append(s)
            top = scores[0].max(axis=-1, keepdims=True)
            for s in scores[1:]:
                top = jnp.maximum(top, s.max(axis=-1, keepdims=True))
            total = jnp.zeros((chunk, 1), F32)
            numer = jnp.zeros((chunk, 2 * HD), F32)
            for t in range(pieces):
                weight = jnp.exp(scores[t] - top)
                total = total + weight.sum(axis=-1, keepdims=True)
                numer = numer + mm(weight.astype(BF), kv_refs[t][1])
            outs.append(numer / total)
            logs.append(top + jnp.log(total))
        att_ref[rows, :] = jnp.where(low, outs[0], outs[1]).astype(BF)
        lse_ref[rows, :] = jnp.where(low, logs[0], logs[1])


def attend(q, kvs, biases):
    n, d = q.shape
    pieces = len(kvs)
    masked = biases is not None
    pair = 2 * HD
    col = pl.BlockSpec((n, pair), lambda j: (0, j))
    kv_spec = pl.BlockSpec((2, n, pair), lambda j: (0, 0, j))
    extra = (biases,) if masked else ()
    return pl.pallas_call(
        partial(attend_kernel, pieces, masked, min(n, 512)),
        name="attend",
        grid=(d // pair,),
        in_specs=[col] + [kv_spec] * pieces + [whole(b.shape) for b in extra],
        out_specs=[col, col],
        out_shape=[jax.ShapeDtypeStruct((n, d), BF), jax.ShapeDtypeStruct((n, d), F32)],
        compiler_params=params_of(("arbitrary",)),
        cost_estimate=pl.CostEstimate(
            flops=4 * n * n * pieces * d, bytes_accessed=(8 + 4 * pieces) * n * d, transcendentals=n * n * pieces * H
        ),
    )(q, *kvs, *extra)


def attend_back_kernel(pieces, masked, *refs):
    q_ref, do_ref, att_ref, lse_ref = refs[:4]
    kv_refs = refs[4 : 4 + pieces]
    refs = refs[4 + pieces :]
    bias_ref = None
    if masked:
        bias_ref, refs = refs[0], refs[1:]
    dq_ref = refs[0]
    dkv_refs = refs[1:]
    n = q_ref.shape[0]
    scale = HD**-0.5
    low = half_masks(n)
    q = q_ref[...] * jnp.asarray(scale, BF)
    do = do_ref[...]
    prod = do.astype(F32) * att_ref[...].astype(F32)
    dq = jnp.zeros((n, 2 * HD), F32)
    qms, doms, deltas, lses = [], [], [], []
    for side in range(2):
        mask = low if side == 0 else ~low
        qms.append(jnp.where(mask, q, jnp.zeros_like(q)))
        doms.append(jnp.where(mask, do, jnp.zeros_like(do)))
        deltas.append(jnp.sum(jnp.where(mask, prod, 0.0), axis=-1, keepdims=True))
        lses.append(lse_ref[:, side * HD : side * HD + 1])
    dqs = [jnp.zeros((n, 2 * HD), F32) for _ in range(2)]
    for t in range(pieces):
        k = kv_refs[t][0]
        v = kv_refs[t][1]
        dk = jnp.zeros((n, 2 * HD), F32)
        dv = jnp.zeros((n, 2 * HD), F32)
        for side in range(2):
            s = mm_nt(qms[side], k)
            if masked:
                s = s + bias_ref[t]
            p = jnp.exp(s - lses[side])
            dp = mm_nt(doms[side], v)
            ds = (p * (dp - deltas[side])).astype(BF)
            dv = dv + mm_tn(p.astype(BF), doms[side])
            dk = dk + mm_tn(ds, qms[side])
            dqs[side] = dqs[side] + mm(ds, k)
        dkv_refs[t][0] = dk.astype(BF)
        dkv_refs[t][1] = dv.astype(BF)
    dq_ref[...] = (jnp.where(low, dqs[0], dqs[1]) * scale).astype(BF)


def attend_back(q, do, att, lse, kvs, biases):
    n, d = q.shape
    pieces = len(kvs)
    masked = biases is not None
    pair = 2 * HD
    col = pl.BlockSpec((n, pair), lambda j: (0, j))
    kv_spec = pl.BlockSpec((2, n, pair), lambda j: (0, 0, j))
    extra = (biases,) if masked else ()
    out = pl.pallas_call(
        partial(attend_back_kernel, pieces, masked),
        name="attend_back",
        grid=(d // pair,),
        in_specs=[col] * 4 + [kv_spec] * pieces + [whole(b.shape) for b in extra],
        out_specs=[col] + [kv_spec] * pieces,
        out_shape=[jax.ShapeDtypeStruct((n, d), BF)] + [jax.ShapeDtypeStruct((2, n, d), BF)] * pieces,
        compiler_params=params_of(("arbitrary",)),
        cost_estimate=pl.CostEstimate(
            flops=10 * n * n * pieces * d, bytes_accessed=(12 + 8 * pieces) * n * d, transcendentals=n * n * pieces * H
        ),
    )(q, do, att, lse, *kvs, *extra)
    return out[0], out[1:]


def normed(value):
    mean = jnp.mean(value, axis=-1, keepdims=True)
    centred = value - mean
    spread = jnp.mean(centred * centred, axis=-1, keepdims=True)
    scale = lax.rsqrt(spread + EPS)
    return centred * scale, scale


def norm_back(grad, xhat, scale):
    mean_grad = jnp.mean(grad, axis=-1, keepdims=True)
    mean_dot = jnp.mean(grad * xhat, axis=-1, keepdims=True)
    return scale * (grad - mean_grad - xhat * mean_dot)


def gelu_pair(value):
    cdf = 0.5 + 0.5 * lax.erf(value * (0.5**0.5))
    pdf = jnp.exp(-0.5 * value * value) * ((2.0 * math.pi) ** -0.5)
    return value * cdf, cdf + value * pdf


def post_kernel(
    x_ref, att_ref, w_ref, e_ref, eb_ref, r_ref, p_ref,
    out_ref, xhat1_ref, scale1_ref, act_ref, slope_ref, xhat2_ref, scale2_ref,
    hidden_ref, low_ref, total_ref,
):
    j = pl.program_id(0)
    lanes = scale1_ref.shape

    @pl.when(j == 0)
    def _():
        summed = x_ref[...].astype(F32) + mm(att_ref[...], w_ref[0]) + p_ref[2:3, :]
        xhat, scale = normed(summed)
        xhat1_ref[...] = xhat
        scale1_ref[...] = jnp.broadcast_to(scale, lanes)
        hidden = xhat * p_ref[3:4, :] + p_ref[4:5, :]
        hidden_ref[...] = hidden
        low_ref[...] = hidden.astype(BF)
        total_ref[...] = jnp.zeros_like(total_ref)

    inner = mm(low_ref[...], e_ref[...]) + eb_ref[...]
    active, slope = gelu_pair(inner)
    active = active.astype(BF)
    act_ref[...] = active
    slope_ref[...] = slope.astype(BF)
    total_ref[...] += mm(active, r_ref[...])

    @pl.when(j == pl.num_programs(0) - 1)
    def _():
        pre = hidden_ref[...] + total_ref[...] + p_ref[5:6, :]
        xhat, scale = normed(pre)
        xhat2_ref[...] = xhat
        scale2_ref[...] = jnp.broadcast_to(scale, lanes)
        out_ref[...] = (xhat * p_ref[6:7, :] + p_ref[7:8, :]).astype(BF)


def post(x, att, w4, e, eb, r, params):
    n, d = x.shape
    ff = e.shape[1]
    fc = min(ff, 512)
    full = whole((n, d))
    thin = whole((n, 128))
    tall = pl.BlockSpec((n, fc), lambda j: (0, j))
    return pl.pallas_call(
        post_kernel,
        name="post",
        grid=(ff // fc,),
        in_specs=[
            full, full,
            pl.BlockSpec((1, d, d), lambda j: (3, 0, 0)),
            pl.BlockSpec((d, fc), lambda j: (0, j)),
            pl.BlockSpec((1, fc), lambda j: (0, j)),
            pl.BlockSpec((fc, d), lambda j: (j, 0)),
            whole(params.shape),
        ],
        out_specs=[full, full, thin, tall, tall, full, thin],
        out_shape=[
            jax.ShapeDtypeStruct((n, d), BF),
            jax.ShapeDtypeStruct((n, d), F32),
            jax.ShapeDtypeStruct((n, 128), F32),
            jax.ShapeDtypeStruct((n, ff), BF),
            jax.ShapeDtypeStruct((n, ff), BF),
            jax.ShapeDtypeStruct((n, d), F32),
            jax.ShapeDtypeStruct((n, 128), F32),
        ],
        scratch_shapes=[pltpu.VMEM((n, d), F32), pltpu.VMEM((n, d), BF), pltpu.VMEM((n, d), F32)],
        compiler_params=params_of(("arbitrary",)),
        cost_estimate=pl.CostEstimate(
            flops=2 * n * d * (d + 2 * ff), bytes_accessed=2 * d * (d + 2 * ff) + 4 * n * ff + 16 * n * d, transcendentals=2 * n * ff
        ),
    )(x, att, w4, e, eb, r, params)


def rows_sum(value):
    return jnp.sum(value, axis=0, keepdims=True)


def ffn_back_kernel(
    g_ref, xhat2_ref, scale2_ref, p_ref, act_ref, slope_ref, r_ref, e_ref, xhat1_ref, scale1_ref, att_ref, w_ref,
    gr_ref, ge_ref, geb_ref, dsum_ref, go_ref, datt_ref, small_ref,
    outer_ref, low_ref, total_ref,
):
    j = pl.program_id(0)

    @pl.when(j == 0)
    def _():
        g = g_ref[...].astype(F32)
        xhat = xhat2_ref[...]
        d_pre = norm_back(g * p_ref[6:7, :], xhat, scale2_ref[:, 0:1])
        outer = d_pre.astype(BF)
        outer_ref[...] = outer
        total_ref[...] = d_pre
        small_ref[0:1, :] = jnp.zeros_like(small_ref[0:1, :])
        small_ref[1:2, :] = jnp.zeros_like(small_ref[1:2, :])
        small_ref[5:6, :] = rows_sum(outer.astype(F32))
        small_ref[6:7, :] = rows_sum(g * xhat)
        small_ref[7:8, :] = rows_sum(g)
        low_ref[...] = (xhat1_ref[...] * p_ref[3:4, :] + p_ref[4:5, :]).astype(BF)

    outer = outer_ref[...]
    d_active = mm_nt(outer, r_ref[...])
    d_inner_full = d_active * slope_ref[...].astype(F32)
    d_inner = d_inner_full.astype(BF)
    gr_ref[...] = mm_tn(act_ref[...], outer).astype(BF)
    ge_ref[...] = mm_tn(low_ref[...], d_inner).astype(BF)
    geb_ref[...] = rows_sum(d_inner.astype(F32))
    total_ref[...] += mm_nt(d_inner, e_ref[...])

    @pl.when(j == pl.num_programs(0) - 1)
    def _():
        d_hidden = total_ref[...]
        xhat = xhat1_ref[...]
        d_summed = norm_back(d_hidden * p_ref[3:4, :], xhat, scale1_ref[:, 0:1])
        dsum_ref[...] = d_summed
        branch = d_summed.astype(BF)
        small_ref[2:3, :] = rows_sum(branch.astype(F32))
        small_ref[3:4, :] = rows_sum(d_hidden * xhat)
        small_ref[4:5, :] = rows_sum(d_hidden)
        go_ref[...] = mm_tn(att_ref[...], branch).astype(BF)
        datt_ref[...] = mm_nt(branch, w_ref[0]).astype(BF)


def ffn_back(g, saved, w4, e, r, params):
    x, att, xhat1, scale1, act, slope, xhat2, scale2 = saved
    n, d = x.shape
    ff = e.shape[1]
    fc = min(ff, 512)
    full = whole((n, d))
    thin = whole((n, 128))
    tall = pl.BlockSpec((n, fc), lambda j: (0, j))
    e_spec = pl.BlockSpec((d, fc), lambda j: (0, j))
    r_spec = pl.BlockSpec((fc, d), lambda j: (j, 0))
    return pl.pallas_call(
        ffn_back_kernel,
        name="ffn_back",
        grid=(ff // fc,),
        in_specs=[
            full, full, thin, whole(params.shape), tall, tall, r_spec, e_spec, full, thin, full,
            pl.BlockSpec((1, d, d), lambda j: (3, 0, 0)),
        ],
        out_specs=[
            r_spec, e_spec, pl.BlockSpec((1, fc), lambda j: (0, j)), full, whole((d, d)), full, whole((8, d)),
        ],
        out_shape=[
            jax.ShapeDtypeStruct((ff, d), BF),
            jax.ShapeDtypeStruct((d, ff), BF),
            jax.ShapeDtypeStruct((1, ff), F32),
            jax.ShapeDtypeStruct((n, d), F32),
            jax.ShapeDtypeStruct((d, d), BF),
            jax.ShapeDtypeStruct((n, d), BF),
            jax.ShapeDtypeStruct((8, d), F32),
        ],
        scratch_shapes=[pltpu.VMEM((n, d), BF), pltpu.VMEM((n, d), BF), pltpu.VMEM((n, d), F32)],
        compiler_params=params_of(("arbitrary",)),
        cost_estimate=pl.CostEstimate(
            flops=4 * n * d * (d + 2 * ff), bytes_accessed=4 * d * (d + 2 * ff) + 4 * n * ff + 24 * n * d, transcendentals=0
        ),
    )(g, xhat2, scale2, params, act, slope, r, e, xhat1, scale1, att, w4)


def input_back_kernel(others, x_ref, dq_ref, own_ref, *refs):
    other_refs = refs[:others]
    w_ref, dsum_ref, g3_ref, dx_ref, small_ref = refs[others:]
    j = pl.program_id(0)

    def step(grad, row):
        g3_ref[0] = mm_tn(x_ref[...], grad).astype(BF)
        if row is not None:
            small_ref[row : row + 1, :] = rows_sum(grad.astype(F32))
        return mm_nt(grad, w_ref[0])

    def joined(index):
        value = own_ref[index].astype(F32)
        for ref in other_refs:
            value = value + ref[index].astype(F32)
        return value.astype(BF)

    @pl.when(j == 0)
    def _():
        small_ref[...] = jnp.zeros_like(small_ref)
        dx_ref[...] = dsum_ref[...] + step(dq_ref[...], 0)

    @pl.when(j == 1)
    def _():
        dx_ref[...] += step(joined(0), None)

    @pl.when(j == 2)
    def _():
        dx_ref[...] += step(joined(1), 1)


def input_back(x, dq, own, others, w4, dsum):
    n, d = x.shape
    full = whole((n, d))
    return pl.pallas_call(
        partial(input_back_kernel, len(others)),
        name="input_back",
        grid=(3,),
        in_specs=[full, full, whole((2, n, d))]
        + [whole((2, n, d))] * len(others)
        + [pl.BlockSpec((1, d, d), lambda j: (j, 0, 0)), full],
        out_specs=[pl.BlockSpec((1, d, d), lambda j: (j, 0, 0)), full, whole((8, d))],
        out_shape=[
            jax.ShapeDtypeStruct((3, d, d), BF),
            jax.ShapeDtypeStruct((n, d), F32),
            jax.ShapeDtypeStruct((8, d), F32),
        ],
        compiler_params=params_of(("arbitrary",)),
        cost_estimate=pl.CostEstimate(flops=12 * n * d * d, bytes_accessed=12 * d * d + 16 * n * d, transcendentals=0),
    )(x, dq, own, *others, w4, dsum)


class Grid:
    def __init__(self, dp, seq):
        self.ny = max(seq // 2, 1)
        self.nc = seq // self.ny
        self.nx = self.ny if dp % self.ny == 0 else 1
        self.nz = dp // self.nx
        self.sizes = {"z": self.nz, "x": self.nx, "y": self.ny, "c": self.nc}

    def here(self):
        d = lax.axis_index("dp")
        s = lax.axis_index("seq")
        return {"z": d // self.nx, "x": lax.rem(d, self.nx), "y": s // self.nc, "c": lax.rem(s, self.nc)}

    def device(self, at):
        return (at["z"] * self.nx + at["x"], at["y"] * self.nc + at["c"])

    def shifted(self, me, axis, step):
        other = dict(me)
        other[axis] = lax.rem(me[axis] + step, self.sizes[axis])
        return other

    def shape(self):
        return (self.nz, self.nx, self.ny, self.nc)

    def peers(self):
        return [(axis, step) for axis in "zxyc" for step in range(1, self.sizes[axis])]

    def barrier(self, me):
        sem = pltpu.get_barrier_semaphore()
        for axis, step in self.peers():
            pl.semaphore_signal(
                sem, inc=1, device_id=self.device(self.shifted(me, axis, step)), device_id_type=MESH
            )
        pl.semaphore_wait(sem, len(self.peers()))


def picked(place, axes):
    return tuple(slice(None) if axis in axes else place[axis] for axis in "zxyc")


def cuts_of(shapes):
    pieces = []
    for number, shape in enumerate(shapes):
        columns = shape[-1]
        if columns % 256 or len(shape) == 2 and shape[0] % 8:
            pieces.append([(number, None, 0, columns)])
            continue
        step = 384 if columns % 384 == 0 else columns // 2
        leads = [None]
        if len(shape) == 3 and shape[0] > 1:
            middle = shape[0] // 2
            leads = [(0, middle), (middle, shape[0])]
        for lead in leads:
            for first in range(0, columns, 2 * step):
                pieces.append([(number, lead, first, step), (number, lead, first + step, step)])
    return pieces


def region(ref, shape, cut, index):
    _, lead, first, count = cut
    head = ()
    if len(shape) == 3:
        head = (slice(None) if lead is None else slice(*lead),)
    return ref.at[head + tuple(index) + (slice(None), slice(first, first + count))]


ORDERS = (("z", "x", "y", "c"), ("z", "y", "x", "c"))


def gather_kernel(grid, shapes, *refs):
    count = len(shapes)
    srcs, dsts = refs[:count], refs[count : 2 * count]
    send_sem, recv_sem, own_sem = refs[2 * count :]
    me = grid.here()
    grid.barrier(me)
    groups = cuts_of(shapes)
    number = [0]
    waits = []

    def send(src, dst, axis, step):
        k = number[0]
        number[0] += 1
        copy = pltpu.make_async_remote_copy(
            src_ref=src, dst_ref=dst, send_sem=send_sem.at[k], recv_sem=recv_sem.at[k],
            device_id=grid.device(grid.shifted(me, axis, step)), device_id_type=MESH,
        )
        copy.start()
        waits.append(copy)
        return copy

    own = []
    first = []
    for group in groups:
        copies = []
        for cut in group:
            shape = shapes[cut[0]]
            src = region(srcs[cut[0]], shape, cut, ())
            dst = region(dsts[cut[0]], shape, cut, picked(me, ""))
            copies.append([send(src, dst, "z", step) for step in range(1, grid.nz)])
        first.append(copies)
    for k in range(count):
        head = (slice(None),) if len(shapes[k]) == 3 else ()
        copy = pltpu.make_async_copy(srcs[k], dsts[k].at[head + picked(me, "")], own_sem.at[k])
        copy.start()
        own.append(copy)
    for copy in own:
        copy.wait()
    stages = {0: first}
    total = len(groups)
    depth = len(ORDERS[0])
    for turn in range(total + depth - 1):
        for stage in range(depth - 1, 0, -1):
            g = turn - (stage - 1)
            if not 0 <= g < total:
                continue
            copies = []
            for side, cut in enumerate(groups[g]):
                order = ORDERS[side % 2]
                for copy in stages[stage - 1][g][side]:
                    copy.wait_recv()
                block = region(dsts[cut[0]], shapes[cut[0]], cut, picked(me, order[:stage]))
                copies.append([send(block, block, order[stage], step) for step in range(1, grid.sizes[order[stage]])])
            stages.setdefault(stage, {})[g] = copies
        g = turn - (depth - 1)
        if 0 <= g < total:
            for copies in stages[depth - 1][g]:
                for copy in copies:
                    copy.wait_recv()
    for copy in waits:
        copy.wait_send()


def copies_in(grid, shapes):
    return sum(len(group) for group in cuts_of(shapes)) * len(grid.peers())


def gather(grid, arrays, name, collective_id):
    shapes = [a.shape for a in arrays]
    outs = [a.shape[:-2] + grid.shape() + a.shape[-2:] for a in arrays]
    count = copies_in(grid, shapes)
    got = pl.pallas_call(
        partial(gather_kernel, grid, shapes),
        name=name,
        in_specs=[pl.BlockSpec(memory_space=pltpu.VMEM)] * len(arrays),
        out_specs=[pl.BlockSpec(memory_space=pl.ANY)] * len(arrays),
        out_shape=[jax.ShapeDtypeStruct(s, a.dtype) for s, a in zip(outs, arrays)],
        scratch_shapes=[
            pltpu.SemaphoreType.DMA((count,)),
            pltpu.SemaphoreType.DMA((count,)),
            pltpu.SemaphoreType.DMA((len(arrays),)),
        ],
        compiler_params=pltpu.CompilerParams(
            collective_id=collective_id, has_side_effects=True, vmem_limit_bytes=VMEM_LIMIT
        ),
    )(*arrays)
    blocks = math.prod(grid.shape())
    return [o.reshape(a.shape[:-2] + (blocks * a.shape[-2], a.shape[-1])) for o, a in zip(got, arrays)]


BACK_ORDERS = (("c", "x", "y", "z"), ("c", "y", "x", "z"))


def left_axes(order, stage):
    return [axis for axis in "zxyc" if axis not in order[:stage]]


def scatter_kernel(grid, shapes, layouts, *refs):
    count = len(shapes)
    srcs, outs = refs[:count], refs[count : 2 * count]
    held = refs[2 * count : 2 * count + sum(len(stages) for stages in layouts)]
    send_sem, recv_sem, own_sem = refs[-3:]
    me = grid.here()
    grid.barrier(me)
    groups = cuts_of(shapes)
    number = [0]
    waits = []
    buffers = {}
    position = 0
    piece = 0
    for g, group in enumerate(groups):
        for side in range(len(group)):
            for stage in range(len(layouts[piece])):
                buffers[g, side, stage] = held[position]
                position += 1
            piece += 1

    def send(src, dst, axis, step):
        k = number[0]
        number[0] += 1
        copy = pltpu.make_async_remote_copy(
            src_ref=src, dst_ref=dst, send_sem=send_sem.at[k], recv_sem=recv_sem.at[k],
            device_id=grid.device(grid.shifted(me, axis, step)), device_id_type=MESH,
        )
        copy.start()
        waits.append(copy)
        return copy

    def part(cut, ref):
        return region(ref, shapes[cut[0]], cut, ())

    owns = {}
    flights = {}
    own_number = 0
    for g, group in enumerate(groups):
        for side, cut in enumerate(group):
            shape = shapes[cut[0]]
            order = BACK_ORDERS[side % 2]
            axis = order[0]
            buf = buffers[g, side, 0]
            mine = dict(me)
            copy = pltpu.make_async_copy(
                region(srcs[cut[0]], shape, cut, picked(mine, "zxy")), buf.at[0], own_sem.at[own_number]
            )
            copy.start()
            owns[g, side] = copy
            own_number += 1
            flights[g, side, 0] = [
                send(
                    region(srcs[cut[0]], shape, cut, picked(grid.shifted(me, axis, step), "zxy")),
                    buf.at[step], axis, step,
                )
                for step in range(1, grid.sizes[axis])
            ]
    depth = 4

    def lead_of(cut):
        return len(shapes[cut[0]]) == 3

    def add_into(buf, cut, stage, order):
        slots = buf.shape[0]
        lead = buf.shape[1] if lead_of(cut) else 1
        spread = buf.shape[2 if lead_of(cut) else 1 : -2]
        blocks = lead * math.prod(spread)
        flat = buf.shape[1:-2]

        def body(i, carry):
            index = []
            rest = i
            for size in reversed(flat):
                index.append(lax.rem(rest, size))
                rest = rest // size
            index = tuple(reversed(index))
            value = buf[(0,) + index].astype(F32)
            for slot in range(1, slots):
                value = value + buf[(slot,) + index].astype(F32)
            buf[(0,) + index] = value.astype(buf.dtype)
            return carry

        lax.fori_loop(0, blocks, body, 0)

    for turn in range(len(groups) + depth - 1):
        for stage in range(depth - 1, -1, -1):
            g = turn - stage
            if not 0 <= g < len(groups):
                continue
            for side, cut in enumerate(groups[g]):
                order = BACK_ORDERS[side % 2]
                buf = buffers[g, side, stage]
                for copy in flights[g, side, stage]:
                    copy.wait_recv()
                if stage == 0:
                    owns[g, side].wait()
                if stage == depth - 1:
                    out = part(cut, outs[cut[0]])
                    value = buffers[g, side, stage - 1]
                    rest = left_axes(order, stage)
                    head = (slice(None),) if lead_of(cut) else ()
                    total = value[(0,) + head + tuple(me[a] for a in rest)].astype(F32)
                    for slot in range(buf.shape[0]):
                        total = total + buf[slot].astype(F32)
                    out[...] = total
                    continue
                if stage == 0:
                    add_into(buf, cut, stage, order)
                    source = buf
                else:
                    source = buffers[g, side, stage - 1]
                    merge(source, buf, me, left_axes(order, stage), order[stage], lead_of(cut), grid)
                    source = buf
                rest = left_axes(order, stage + 1)
                axis = order[stage + 1]
                nxt = buffers[g, side, stage + 1]
                head = (slice(None),) if lead_of(cut) else ()
                flights[g, side, stage + 1] = []
                base = 0 if stage + 1 == depth - 1 else 1
                for step in range(1, grid.sizes[axis]):
                    there = grid.shifted(me, axis, step)
                    index = tuple(there[a] if a == axis else slice(None) for a in rest)
                    flights[g, side, stage + 1].append(
                        send(source.at[(0,) + head + index], nxt.at[step - 1 + base], axis, step)
                    )
    for copy in waits:
        copy.wait_send()


def merge(source, buf, me, axes, axis, lead, grid):
    flat = buf.shape[1:-2]
    blocks = math.prod(flat) if flat else 1
    where = axes.index(axis) + (1 if lead else 0)

    def body(i, carry):
        index = []
        rest = i
        for size in reversed(flat):
            index.append(lax.rem(rest, size))
            rest = rest // size
        index = tuple(reversed(index))
        wide = index[:where] + (me[axis],) + index[where:]
        value = source[(0,) + wide].astype(F32)
        for slot in range(1, buf.shape[0]):
            value = value + buf[(slot,) + index].astype(F32)
        buf[(0,) + index] = value.astype(buf.dtype)
        return carry

    lax.fori_loop(0, blocks, body, 0)


def scatter(grid, arrays, name, collective_id):
    blocks = math.prod(grid.shape())
    shapes = [a.shape[:-2] + (a.shape[-2] // blocks, a.shape[-1]) for a in arrays]
    views = [a.reshape(s[:-2] + grid.shape() + s[-2:]) for a, s in zip(arrays, shapes)]
    layouts = []
    scratch = []
    pieces = 0
    for group in cuts_of(shapes):
        for side, cut in enumerate(group):
            shape = shapes[cut[0]]
            order = BACK_ORDERS[side % 2]
            head = ()
            if len(shape) == 3:
                head = (shape[0] if cut[1] is None else cut[1][1] - cut[1][0],)
            stages = []
            for stage in range(4):
                rest = left_axes(order, stage + 1)
                slots = grid.sizes[order[stage]] - (1 if stage == 3 else 0)
                stages.append((slots,) + head + tuple(grid.sizes[a] for a in rest) + (shape[-2], cut[3]))
            layouts.append(stages)
            scratch += [pltpu.VMEM(s, arrays[cut[0]].dtype) for s in stages]
            pieces += 1
    count = copies_in(grid, shapes)
    return pl.pallas_call(
        partial(scatter_kernel, grid, shapes, layouts),
        name=name,
        in_specs=[pl.BlockSpec(memory_space=pl.ANY)] * len(arrays),
        out_specs=[pl.BlockSpec(memory_space=pltpu.VMEM)] * len(arrays),
        out_shape=[jax.ShapeDtypeStruct(s, F32) for s in shapes],
        scratch_shapes=scratch
        + [
            pltpu.SemaphoreType.DMA((count,)),
            pltpu.SemaphoreType.DMA((count,)),
            pltpu.SemaphoreType.DMA((pieces,)),
        ],
        compiler_params=pltpu.CompilerParams(
            collective_id=collective_id, has_side_effects=True, vmem_limit_bytes=VMEM_LIMIT
        ),
    )(*views)


ROWS = 8
ROW_AT = (1, 4, 6, 7, 8, 12, 13, 14)


def pack_small(layers):
    parts = []
    for params in layers:
        parts += [params[k] for k in ROW_AT] + [params[10]]
    flat = jnp.concatenate(parts)
    size = 1024 * -(-flat.shape[0] // 1024)
    return jnp.pad(flat, (0, size - flat.shape[0])).reshape(size // 128, 128)


def unpack_small(full, blocks, rows, layers):
    per = full.shape[0] // blocks * full.shape[1]
    flat = full.reshape(blocks, per)
    out = []
    width = (ROWS + 4) * rows
    for layer in range(layers):
        part = flat[:, layer * width : (layer + 1) * width].astype(F32)
        thin = part[:, : ROWS * rows].reshape(blocks, ROWS, rows).transpose(1, 0, 2).reshape(ROWS, blocks * rows)
        out.append((thin, part[:, ROWS * rows :].reshape(1, blocks * 4 * rows)))
    return out


def pack_grads(grads, blocks, rows):
    parts = []
    for thin, wide in grads:
        parts.append(thin.reshape(ROWS, blocks, rows).transpose(1, 0, 2).reshape(blocks, ROWS * rows))
        parts.append(wide.reshape(blocks, 4 * rows))
    flat = jnp.concatenate(parts, axis=1)
    size = 1024 * -(-flat.shape[1] // 1024)
    return jnp.pad(flat, ((0, 0), (0, size - flat.shape[1]))).reshape(blocks * (size // 128), 128)


def on_device(grid, tokens, early, cot_backbone, cot_head, lengths, cls_pos, *weights):
    layers = (weights[:15], weights[15:])
    members = lax.axis_size("seq")
    blocks = math.prod(grid.shape())
    seqs, rows, width = tokens.shape
    half = members // seqs
    spot = lax.axis_index("seq")
    mine = spot // half
    swap = [(i, (i + half) % members) for i in range(members)]
    far = lax.rem(spot + half, members)
    masked = rows * members > MIN_LEN

    def spread(value):
        kept = lax.dynamic_index_in_dim(value, mine, 0, keepdims=False)
        sent = lax.dynamic_index_in_dim(value, 1 - mine, 0, keepdims=False)
        return jnp.concatenate([kept, lax.ppermute(sent, "seq", swap)], axis=0)

    def collect(value):
        kept = value[:rows]
        got = lax.ppermute(value[rows:], "seq", swap)
        return jnp.where(mine == 0, jnp.stack([kept, got]), jnp.stack([got, kept]))

    def around(value, step):
        pairs = [(i, i // half * half + (i % half + step) % half) for i in range(members)]
        return lax.ppermute(value, "seq", pairs)

    length = lax.dynamic_index_in_dim(lengths, mine, 0, keepdims=False)
    cls = lax.dynamic_index_in_dim(cls_pos, mine, 0, keepdims=False)
    line = jnp.arange(rows, dtype=jnp.int32)
    positions = jnp.concatenate([spot * rows + line, far * rows + line])
    is_cls = (positions == cls)[:, None]
    valid = (positions < length)[:, None]
    biases = None
    if masked:
        steps = []
        for step in range(half):
            member = mine * half + lax.rem(lax.rem(spot, half) - step + half, half)
            other = lax.rem(member + half, members)
            place = jnp.concatenate([member * rows + line, other * rows + line])
            steps.append(jnp.where(place < length, 0.0, NEG)[None, :])
        biases = jnp.stack(steps)

    x_back = spread(tokens)
    x_early = spread(early)
    g_back = spread(cot_backbone)
    g_head = spread(cot_head)
    if masked:
        g_back = jnp.where(valid, g_back, jnp.zeros_like(g_back))
        g_head = jnp.where(valid, g_head, jnp.zeros_like(g_head))

    shard = layers[0][0].shape[0]
    stacked = [jnp.stack([p[0], p[2], p[3], p[5]]) for p in layers]
    small = pack_small(layers)
    w4_back, e_back, r_back, small_full = gather(
        grid, [stacked[0], layers[0][9], layers[0][11], small], "gather_back", 0
    )
    w4_head, e_head, r_head = gather(grid, [stacked[1], layers[1][9], layers[1][11]], "gather_head", 1)
    (p_back, eb_back), (p_head, eb_head) = unpack_small(small_full, blocks, shard, 2)

    def forward(x, w4, e, r, params, eb):
        q, kv = qkv(x, w4, params)
        kvs = [kv] + [around(kv, step) for step in range(1, half)]
        att, lse = attend(q, kvs, biases)
        out, xhat1, scale1, act, slope, xhat2, scale2 = post(x, att, w4, e, eb, r, params)
        return out, (q, kvs, lse, (x, att, xhat1, scale1, act, slope, xhat2, scale2))

    def backward(g, kept, w4, e, r, params):
        q, kvs, lse, saved = kept
        x, att = saved[:2]
        gr, ge, geb, dsum, go, datt, small_a = ffn_back(g, saved, w4, e, r, params)
        dq, dkvs = attend_back(q, datt, att, lse, kvs, biases)
        others = [around(dkvs[step], half - step) for step in range(1, half)]
        g3, dx, small_b = input_back(x, dq, dkvs[0], others, w4, dsum)
        return dx, (g3, go[None], ge, gr), (small_a + small_b, geb)

    back_low, back_kept = forward(x_back, w4_back, e_back, r_back, p_back, eb_back)
    head_in = jnp.where(is_cls, back_low, x_early)
    head_low, head_kept = forward(head_in, w4_head, e_head, r_head, p_head, eb_head)
    dx_head, big_head, small_head = backward(g_head, head_kept, w4_head, e_head, r_head, p_head)
    s3h, soh, seh, srh = scatter(grid, list(big_head), "scatter_head", 2)
    g_mixed = g_back.astype(F32) + jnp.where(is_cls, dx_head, 0.0)
    dx_back, big_back, small_back = backward(g_mixed, back_kept, w4_back, e_back, r_back, p_back)
    packed = pack_grads([small_back, small_head], blocks, shard)
    s3b, sob, seb, srb, small_sum = scatter(grid, list(big_back) + [packed], "scatter_back", 3)

    flat = small_sum.reshape(-1)

    def layer_grads(layer, s3, so, se, sr):
        base = layer * (ROWS + 4) * shard
        thin = [flat[base + k * shard : base + (k + 1) * shard] for k in range(ROWS)]
        wide = flat[base + ROWS * shard : base + (ROWS + 4) * shard]
        return (
            s3[0], thin[0], s3[1], s3[2], thin[1], so[0], thin[2], thin[3], thin[4],
            se, wide, sr, thin[5], thin[6], thin[7],
        )

    return (
        collect(back_low),
        collect(head_low),
        collect(dx_back.astype(BF)),
        collect(jnp.where(is_cls, 0.0, dx_head).astype(BF)),
    ) + layer_grads(0, s3b, sob, seb, srb) + layer_grads(1, s3h, soh, seh, srh)


def solution(mesh):
    rows = P("dp", "seq", None)
    wide = P(("dp", "seq"), None)
    thin = P(("dp", "seq"))
    layer = tuple(thin if k in (1, 4, 6, 7, 8, 10, 12, 13, 14) else wide for k in range(15))
    grid = Grid(mesh.shape["dp"], mesh.shape["seq"])
    return jax.shard_map(
        partial(on_device, grid),
        mesh=mesh,
        in_specs=(rows,) * 4 + (P("dp"),) * 2 + layer + layer,
        out_specs=(rows,) * 4 + layer + layer,
        check_vma=False,
    )
```

time: 2870 us -> 617 us (0.21)
  waiting for transfers between devices: 2120 us -> 24.2 us
  Pallas kernels: 0 us -> 535 us
  matrix products: 369 us -> 0 us
  local copies, waits for them, and re-layouts: 189 us -> 20.9 us
  other arithmetic: 112 us -> 16.3 us
  blocking collectives: 40.9 us -> 0 us
    reduce_scatter x17 -> x0, waiting for transfers between devices: 1160 us -> none  [the longest x1 142 us: on_device(): lax.psum_scatter(combined[24], ('dp', 'seq'), scatter_dimension=0, tiled=...]
    pallas_call x0 -> x16, Pallas kernels: none -> 535 us  [the longest x2 181 us: scatter(): pl.pallas_call(partial(scatter_kernel, grid, shapes, layouts), name=name,...]
    all_gather x20 -> x0, waiting for transfers between devices: 532 us -> none  [the longest x2 106 us: gather_layer(): lax.all_gather(params[2], ('dp', 'seq'), axis=0, tiled=True)]
    unnamed x45 -> x0, waiting for transfers between devices: 420 us -> none
    dot_general x128 -> x0, matrix products: 369 us -> none  [the longest x24 87.1 us: product(): return jnp.dot(left, right, preferred_element_type=jnp.float32)]
    unnamed x599 -> x100, local copies, waits for them, and re-layouts: 82.9 us -> 7.03 us
    reduce_sum x41 -> x0, other arithmetic: 60 us -> none  [the longest x8 31.7 us: forward_step(): total = total * decay + jnp.sum(weight, axis=-1)]
    unnamed x1 -> x0, blocking collectives: 40.9 us -> none
  transfers between devices with their start and end apart: 41 -> 12, of which waited for: 35 -> 4; matrix products, arithmetic and copies ran while one was open for 17% -> 4% of each run, Pallas kernels for 0% -> 64%
where the time goes in v1:
time: 617 us; the launch traced here: 613 us
  Pallas kernels  535 us (87%)
  waiting for transfers between devices  24.2 us (4%)
  local copies, waits for them, and re-layouts  20.9 us (3%)
  other arithmetic  16.3 us (3%)
  starting transfers between devices  14.5 us (2%)
    pallas_call x2, Pallas kernels, scatter(): pl.pallas_call(partial(scatter_kernel, grid, shapes, layouts), name=name,...  181 us
    pallas_call x2, Pallas kernels, gather(): pl.pallas_call(partial(gather_kernel, grid, shapes), name=name, in_specs=...  175 us
    pallas_call x2, Pallas kernels, attend_back(): pl.pallas_call(partial(attend_back_kernel, pieces, masked), name='attend_...  46.1 us
    pallas_call x2, Pallas kernels, ffn_back(): pl.pallas_call(ffn_back_kernel, name='ffn_back', grid=(ff // fc,), in_spe...  43.3 us
    pallas_call x2, Pallas kernels, post(): pl.pallas_call(post_kernel, name='post', grid=(ff // fc,), in_specs=[full...  31.3 us
    pallas_call x2, Pallas kernels, attend(): pl.pallas_call(partial(attend_kernel, pieces, masked, min(n, 512)), name=...  27.6 us
    pallas_call x2, Pallas kernels, input_back(): pl.pallas_call(partial(input_back_kernel, len(others)), name='input_back'...  18.8 us
    ppermute x4, waiting for transfers between devices, collect(): got = lax.ppermute(value[rows:], 'seq', swap)  13.9 us
  transfers between devices with their start and end apart: 12, of which 4 were waited for; matrix products, arithmetic and copies ran while one was open for 4% of the time, Pallas kernels for 64%

profile of v1, /device:TPU:0, one launch (start us, length us, event | category | flops | bytes accessed | tf_op | source)
XLA Modules:
  0.0 613.0 jit_solution(15383461812193797251)
XLA Ops:
  2.2 3.1 collective-permute-start
  6.8 85.8 %gather_back.1 = (bf16[4,4,2,2,2,24,768]{6,5,4,3,2,1,0:T(8,128)(2,1)}, bf16[4,2,2,2,24,3072]{5,4,3,2,1,0:T(8,128)(2,1)}, bf16[4,2,2,2,96,768]{5,4,3,2,1,0:T(8,128)(2,1)}, bf16[4,2,2,2,8,128]{5,4,3,2,1,0:T(8,128)(2,1)}) custom-call(bf16[4,24,768]{2,1,0:T(8,128)(2,1)} %pad_maximum_fusion.2.refs_0_, bf16[24,3072]{1,0:T(8,128)(2,1)} %refs_1_.2, ...), custom_call_target="tpu_custom_call" | custom-call | tf_op jit(solution)/shard_map/gather_back/pallas_call | solution.py:586
  95.4 6.1 %qkv.2 = (bf16[512,768]{1,0:T(8,128)(2,1)}, bf16[2,512,768]{2,1,0:T(8,128)(2,1)}) custom-call(bf16[512,768]{1,0:T(8,128)(2,1)} %pad_maximum_fusion.x_ref, bf16[4,768,768]{2,1,0:T(8,128)(2,1)} %bitcast.112, f32[8,768]{1,0:T(8,128)} %reshape.162.p_ref), custom_call_target="tpu_custom_call" | custom-call | flops 1811939328 | bytes 6684672 | tf_op jit(solution)/shard_map/qkv/pallas_call | solution.py:61
  105.9 89.2 %gather_head.1 = (bf16[4,4,2,2,2,24,768]{6,5,4,3,2,1,0:T(8,128)(2,1)}, bf16[4,2,2,2,24,3072]{5,4,3,2,1,0:T(8,128)(2,1)}, bf16[4,2,2,2,96,768]{5,4,3,2,1,0:T(8,128)(2,1)}) custom-call(bf16[4,24,768]{2,1,0:T(8,128)(2,1)} %pad_maximum_fusion.3.refs_0_, bf16[24,3072]{1,0:T(8,128)(2,1)} %refs_1_.3, bf16[96,768]{1,0:T(8,128)(2,1)} %refs_2_.3), custom_call_target="tpu_custom_call" | custom-call | tf_op jit(solution)/shard_map/gather_head/pallas_call | solution.py:586
  195.9 13.8 %attend.2 = (bf16[512,768]{1,0:T(8,128)(2,1)}, f32[512,768]{1,0:T(8,128)}) custom-call(bf16[512,768]{1,0:T(8,128)(2,1)} %get-tuple-element.100.refs_0_, bf16[2,512,768]{2,1,0:T(8,128)(2,1)} %get-tuple-element.101.refs_1_.refs_4_, bf16[2,512,768]{2,1,0:T(8,128)(2,1)} %collective-permute-done.1.refs_2_.refs_5_), custom_call_target="tpu_custom_call" | custom-call | flops 1610612736 | bytes 6291456 | tf_op jit(solution)/shard_map/attend/pallas_call | solution.py:134
  209.7 15.6 %post.2 = (bf16[512,768]{1,0:T(8,128)(2,1)}, f32[512,768]{1,0:T(8,128)}, f32[512,128]{1,0:T(8,128)}, bf16[512,3072]{1,0:T(8,128)(2,1)}, bf16[512,3072]{1,0:T(8,1...) custom-call(bf16[512,768]{1,0:T(8,128)(2,1)} %pad_maximum_fusion.x_ref, ...), custom_call_target="tpu_custom_call" | custom-call | flops 5435817984 | bytes 23199744 | tf_op jit(solution)/shard_map/post/pallas_call | solution.py:277
  225.3 2.3 maximum_select_fusion.1.x_ref
  227.6 5.8 qkv.3
  233.9 3.3 collective-permute-start.7
  238.0 8.5 %collective-permute-done.7 = bf16[256,768]{1,0:T(8,128)(2,1)S(1)} collective-permute-done((bf16[256,768]{1,0:T(8,128)(2,1)S(1)}, bf16[256,768]{1,0:T(8,128)(2,1)S(1)}, u32[]{:S(2)}, u32[]{:S(2)}) %collective-permute-start.7) | collective-permute-done | bytes 393248 | tf_op jit(solution)/shard_map/ppermute | solution.py:854
  247.5 13.8 %attend.3 = (bf16[512,768]{1,0:T(8,128)(2,1)}, f32[512,768]{1,0:T(8,128)}) custom-call(bf16[512,768]{1,0:T(8,128)(2,1)} %get-tuple-element.107.refs_0_, bf16[2,512,768]{2,1,0:T(8,128)(2,1)} %get-tuple-element.108.refs_1_.refs_4_, bf16[2,512,768]{2,1,0:T(8,128)(2,1)} %collective-permute-done.4.refs_2_.refs_5_), custom_call_target="tpu_custom_call" | custom-call | flops 1610612736 | bytes 6291456 | tf_op jit(solution)/shard_map/attend/pallas_call | solution.py:134
  261.4 15.7 %post.3 = (bf16[512,768]{1,0:T(8,128)(2,1)}, f32[512,768]{1,0:T(8,128)}, f32[512,128]{1,0:T(8,128)}, bf16[512,3072]{1,0:T(8,128)(2,1)}, bf16[512,3072]{1,0:T(8,1...) custom-call(bf16[512,768]{1,0:T(8,128)(2,1)} %maximum_select_fusion.1.x_ref, ...), custom_call_target="tpu_custom_call" | custom-call | flops 5435817984 | bytes 23199744 | tf_op jit(solution)/shard_map/post/pallas_call | solution.py:277
  277.1 21.5 %ffn_back.2 = (bf16[3072,768]{1,0:T(8,128)(2,1)}, bf16[768,3072]{1,0:T(8,128)(2,1)}, f32[1,3072]{1,0:T(1,128)}, f32[512,768]{1,0:T(8,128)}, bf16[768,768]{1,0:T(...) custom-call(bf16[512,768]{1,0:T(8,128)(2,1)} %pad_maximum_fusion.1.g_ref, ...), custom_call_target="tpu_custom_call" | custom-call | flops 10871635968 | bytes 36962304 | tf_op jit(solution)/shard_map/ffn_back/pallas_call | solution.py:366
  298.7 22.9 %attend_back.2 = (bf16[512,768]{1,0:T(8,128)(2,1)}, bf16[2,512,768]{2,1,0:T(8,128)(2,1)}, bf16[2,512,768]{2,1,0:T(8,128)(2,1)}) custom-call(bf16[512,768]{1,0:T(8,128)(2,1)} %get-tuple-element.107.refs_0_, bf16[512,768]{1,0:T(8,128)(2,1)} %get-tuple-element.119.refs_1_, bf16[512,768]{1,0:T(8,128)(2,1)} %get-tuple-element.109.att_ref.refs_2_, ...), custom_call_target="tpu_custom_call" | custom-call | flops 4026531840 | bytes 11010048 | tf_op jit(solution)/shard_map/attend_back/pallas_call | solution.py:200
  326.5 9.5 %input_back.2 = (bf16[3,768,768]{2,1,0:T(8,128)(2,1)}, f32[512,768]{1,0:T(8,128)}, f32[8,768]{1,0:T(8,128)}) custom-call(bf16[512,768]{1,0:T(8,128)(2,1)} %maximum_select_fusion.1.x_ref, bf16[512,768]{1,0:T(8,128)(2,1)} %get-tuple-element.121.dq_ref, bf16[2,512,768]{2,1,0:T(8,128)(2,1)} %get-tuple-element.122.own_ref, bf16[2,512,768]{2,1,0:T(8,128)(2,1)} %copy-done.44, ...), custom_call_target="tpu_custom_call" | custom-call | flops 3623878656 | bytes 13369344 | tf_op jit(solution)/shard_map/input_back/pallas_call | solution.py:428
  336.0 2.8 select_add_fusion.g_ref
  338.8 21.7 %ffn_back.3 = (bf16[3072,768]{1,0:T(8,128)(2,1)}, bf16[768,3072]{1,0:T(8,128)(2,1)}, f32[1,3072]{1,0:T(1,128)}, f32[512,768]{1,0:T(8,128)}, bf16[768,768]{1,0:T(...) custom-call(f32[512,768]{1,0:T(8,128)} %select_add_fusion.g_ref, f32[512,768]{1,0:T(8,128)} %get-tuple-element.126.xhat2_ref, ...), custom_call_target="tpu_custom_call" | custom-call | flops 10871635968 | bytes 36962304 | tf_op jit(solution)/shard_map/ffn_back/pallas_call | solution.py:366
  360.6 23.2 %attend_back.3 = (bf16[512,768]{1,0:T(8,128)(2,1)}, bf16[2,512,768]{2,1,0:T(8,128)(2,1)}, bf16[2,512,768]{2,1,0:T(8,128)(2,1)}) custom-call(bf16[512,768]{1,0:T(8,128)(2,1)} %get-tuple-element.100.refs_0_, bf16[512,768]{1,0:T(8,128)(2,1)} %get-tuple-element.132.refs_1_, bf16[512,768]{1,0:T(8,128)(2,1)} %get-tuple-element.102.att_ref.refs_2_, ...), custom_call_target="tpu_custom_call" | custom-call | flops 4026531840 | bytes 11010048 | tf_op jit(solution)/shard_map/attend_back/pallas_call | solution.py:200
  388.3 7.8 %collective-permute-done.2 = bf16[256,768]{1,0:T(8,128)(2,1)S(1)} collective-permute-done((bf16[256,768]{1,0:T(8,128)(2,1)S(1)}, bf16[256,768]{1,0:T(8,128)(2,1)S(1)}, u32[]{:S(2)}, u32[]{:S(2)}) %collective-permute-start.2) | collective-permute-done | bytes 393248 | tf_op jit(solution)/shard_map/ppermute | solution.py:858
  398.4 6.1 %collective-permute-done.5 = bf16[256,768]{1,0:T(8,128)(2,1)S(1)} collective-permute-done((bf16[256,768]{1,0:T(8,128)(2,1)S(1)}, bf16[256,768]{1,0:T(8,128)(2,1)S(1)}, u32[]{:S(2)}, u32[]{:S(2)}) %collective-permute-start.5) | collective-permute-done | bytes 393248 | tf_op jit(solution)/shard_map/ppermute | solution.py:858
  406.6 87.0 %scatter_head.1 = (f32[3,24,768]{2,1,0:T(8,128)}, f32[1,24,768]{2,1,0:T(8,128)}, f32[24,3072]{1,0:T(8,128)}, f32[96,768]{1,0:T(8,128)}) custom-call(bf16[3,4,2,2,2,24,768]{6,5,4,3,2,1,0:T(8,128)(2,1)} %bitcast.85, bf16[1,4,2,2,2,24,768]{6,5,4,3,2,1,0:T(8,128)(2,1)} %bitcast.87, bf16[4,2,2,2,24,3072]{5,4,3,2,1,0:T(8,128)(2,1)} %bitcast.82, ...), custom_call_target="tpu_custom_call" | custom-call | tf_op jit(solution)/shard_map/scatter_head/pallas_call | solution.py:786
  496.3 9.3 %input_back.3 = (bf16[3,768,768]{2,1,0:T(8,128)(2,1)}, f32[512,768]{1,0:T(8,128)}, f32[8,768]{1,0:T(8,128)}) custom-call(bf16[512,768]{1,0:T(8,128)(2,1)} %pad_maximum_fusion.x_ref, bf16[512,768]{1,0:T(8,128)(2,1)} %get-tuple-element.134.dq_ref, bf16[2,512,768]{2,1,0:T(8,128)(2,1)} %get-tuple-element.135.own_ref, ...), custom_call_target="tpu_custom_call" | custom-call | flops 3623878656 | bytes 13369344 | tf_op jit(solution)/shard_map/input_back/pallas_call | solution.py:428
  508.4 94.0 %scatter_back.1 = (f32[3,24,768]{2,1,0:T(8,128)}, f32[1,24,768]{2,1,0:T(8,128)}, f32[24,3072]{1,0:T(8,128)}, f32[96,768]{1,0:T(8,128)}, f32[8,128]{1,0:T(8,128)}) custom-call(bf16[3,4,2,2,2,24,768]{6,5,4,3,2,1,0:T(8,128)(2,1)} %bitcast.86, bf16[1,4,2,2,2,24,768]{6,5,4,3,2,1,0:T(8,128)(2,1)} %bitcast.88, bf16[4,2,2,2,24,3072]{5,4,3,2,1,0:T(8,128)(2,1)} %bitcast.84, ...), custom_call_target="tpu_custom_call" | custom-call | tf_op jit(solution)/shard_map/scatter_back/pallas_call | solution.py:786
  602.5 1.9 fusion.1
  (172 shorter events, 39.9 us)
Async XLA Ops:
  0.9 5.3 copy-start.12
  2.2 92.2 %collective-permute-start = (bf16[256,768]{1,0:T(8,128)(2,1)S(1)}, bf16[256,768]{1,0:T(8,128)(2,1)S(1)}, u32[]{:S(2)}, u32[]{:S(2)}) collective-permute-start(bf16[256,768]{1,0:T(8,128)(2,1)S(1)} %get-tuple-element.177), channel_id=1, source_target_pairs={{0,2},{1,3},{2,0},{3,1},{4,6},{5,7},{6,4},{7,5},{8,10},{9,11},{10,... | collective-permute-start | bytes 1179656 | tf_op jit(solution)/shard_map/ppermute | solution.py:854
  95.4 6.8 %copy-start.3 = (bf16[2,256,768]{2,1,0:T(8,128)(2,1)S(1)}, bf16[2,256,768]{2,1,0:T(8,128)(2,1)}, u32[]{:S(2)}) copy-start(bf16[2,256,768]{2,1,0:T(8,128)(2,1)} %param.37) | copy-start | bytes 2359300
  101.5 94.3 %collective-permute-start.1 = (bf16[2,512,768]{2,1,0:T(8,128)(2,1)}, bf16[2,512,768]{2,1,0:T(8,128)(2,1)}, u32[]{:S(2)}, u32[]{:S(2)}) collective-permute-start(bf16[2,512,768]{2,1,0:T(8,128)(2,1)} %get-tuple-element.101.refs_1_.refs_4_), channel_id=1, source_target_pairs={{0,1},{1,0},{2,3},{3,2},{4,5},{5,4},{6,7},{7,6},{8,9},{9,8},{10,11... | collective-permute-start | bytes 4718600 | tf_op jit(solution)/shard_map/ppermute | solution.py:863
  102.2 123.1 %collective-permute-start.3 = (bf16[256,768]{1,0:T(8,128)(2,1)S(1)}, bf16[256,768]{1,0:T(8,128)(2,1)S(1)}, u32[]{:S(2)}, u32[]{:S(2)}) collective-permute-start(bf16[256,768]{1,0:T(8,128)(2,1)S(1)} %get-tuple-element.173), channel_id=1, source_target_pairs={{0,2},{1,3},{2,0},{3,1},{4,6},{5,7},{6,4},{7,5},{8,10},{9,11},{10,... | collective-permute-start | bytes 1179656 | tf_op jit(solution)/shard_map/ppermute | solution.py:854
  227.6 6.3 %copy-start.4 = (bf16[2,256,768]{2,1,0:T(8,128)(2,1)S(1)}, bf16[2,256,768]{2,1,0:T(8,128)(2,1)}, u32[]{:S(2)}) copy-start(bf16[2,256,768]{2,1,0:T(8,128)(2,1)} %param.39) | copy-start | bytes 2359300
  233.4 14.2 %collective-permute-start.4 = (bf16[2,512,768]{2,1,0:T(8,128)(2,1)}, bf16[2,512,768]{2,1,0:T(8,128)(2,1)}, u32[]{:S(2)}, u32[]{:S(2)}) collective-permute-start(bf16[2,512,768]{2,1,0:T(8,128)(2,1)} %get-tuple-element.108.refs_1_.refs_4_), channel_id=1, source_target_pairs={{0,1},{1,0},{2,3},{3,2},{4,5},{5,4},{6,7},{7,6},{8,9},{9,8},{10,11... | collective-permute-start | bytes 4718600 | tf_op jit(solution)/shard_map/ppermute | solution.py:863
  233.9 12.6 %collective-permute-start.7 = (bf16[256,768]{1,0:T(8,128)(2,1)S(1)}, bf16[256,768]{1,0:T(8,128)(2,1)S(1)}, u32[]{:S(2)}, u32[]{:S(2)}) collective-permute-start(bf16[256,768]{1,0:T(8,128)(2,1)S(1)} %get-tuple-element.169), channel_id=1, source_target_pairs={{0,2},{1,3},{2,0},{3,1},{4,6},{5,7},{6,4},{7,5},{8,10},{9,11},{10,... | collective-permute-start | bytes 1179656 | tf_op jit(solution)/shard_map/ppermute | solution.py:854
  298.6 23.0 %copy-start.5 = (bf16[2,256,768]{2,1,0:T(8,128)(2,1)S(1)}, bf16[2,256,768]{2,1,0:T(8,128)(2,1)}, u32[]{:S(2)}) copy-start(bf16[2,256,768]{2,1,0:T(8,128)(2,1)} %param.38) | copy-start | bytes 2359300
  321.6 3.7 collective-permute-start.8
  321.8 14.2 %collective-permute-start.6 = (bf16[256,768]{1,0:T(8,128)(2,1)S(1)}, bf16[256,768]{1,0:T(8,128)(2,1)S(1)}, u32[]{:S(2)}, u32[]{:S(2)}) collective-permute-start(bf16[256,768]{1,0:T(8,128)(2,1)S(1)} %get-tuple-element.167), channel_id=1, source_target_pairs={{0,2},{1,3},{2,0},{3,1},{4,6},{5,7},{6,4},{7,5},{8,10},{9,11},{10,... | collective-permute-start | bytes 1179656 | tf_op jit(solution)/shard_map/ppermute | solution.py:854
  360.6 23.4 %copy-start.1 = (bf16[512,768]{1,0:T(8,128)(2,1)S(1)}, bf16[512,768]{1,0:T(8,128)(2,1)}, u32[]{:S(2)}) copy-start(bf16[512,768]{1,0:T(8,128)(2,1)} %get-tuple-element.105) | copy-start | bytes 2359300
  383.8 112.5 %collective-permute-start.9 = (bf16[2,512,768]{2,1,0:T(8,128)(2,1)}, bf16[2,512,768]{2,1,0:T(8,128)(2,1)}, u32[]{:S(2)}, u32[]{:S(2)}) collective-permute-start(bf16[2,512,768]{2,1,0:T(8,128)(2,1)} %get-tuple-element.136), channel_id=1, source_target_pairs={{0,1},{1,0},{2,3},{3,2},{4,5},{5,4},{6,7},{7,6},{8,9},{9,8},{10,11... | collective-permute-start | bytes 4718600 | tf_op jit(solution)/shard_map/ppermute | solution.py:863
  384.1 12.1 %collective-permute-start.2 = (bf16[256,768]{1,0:T(8,128)(2,1)S(1)}, bf16[256,768]{1,0:T(8,128)(2,1)S(1)}, u32[]{:S(2)}, u32[]{:S(2)}) collective-permute-start(bf16[256,768]{1,0:T(8,128)(2,1)S(1)} %get-tuple-element.175), channel_id=1, source_target_pairs={{0,2},{1,3},{2,0},{3,1},{4,6},{5,7},{6,4},{7,5},{8,10},{9,11},{10,... | collective-permute-start | bytes 1179656 | tf_op jit(solution)/shard_map/ppermute | solution.py:858
  385.9 18.6 %collective-permute-start.5 = (bf16[256,768]{1,0:T(8,128)(2,1)S(1)}, bf16[256,768]{1,0:T(8,128)(2,1)S(1)}, u32[]{:S(2)}, u32[]{:S(2)}) collective-permute-start(bf16[256,768]{1,0:T(8,128)(2,1)S(1)} %get-tuple-element.171), channel_id=1, source_target_pairs={{0,2},{1,3},{2,0},{3,1},{4,6},{5,7},{6,4},{7,5},{8,10},{9,11},{10,... | collective-permute-start | bytes 1179656 | tf_op jit(solution)/shard_map/ppermute | solution.py:858
  386.9 10.7 %copy-start.24 = (f32[1,3072]{1,0:T(1,128)S(1)}, f32[1,3072]{1,0:T(1,128)}, u32[]{:S(2)}) copy-start(f32[1,3072]{1,0:T(1,128)} %get-tuple-element.148) | copy-start | bytes 36868
  387.0 108.3 %collective-permute-start.11 = (bf16[256,768]{1,0:T(8,128)(2,1)S(1)}, bf16[256,768]{1,0:T(8,128)(2,1)S(1)}, u32[]{:S(2)}, u32[]{:S(2)}) collective-permute-start(bf16[256,768]{1,0:T(8,128)(2,1)S(1)} %get-tuple-element.163), channel_id=1, source_target_pairs={{0,2},{1,3},{2,0},{3,1},{4,6},{5,7},{6,4},{7,5},{8,10},{9,11},{10,... | collective-permute-start | bytes 1179656 | tf_op jit(solution)/shard_map/ppermute | solution.py:858
  396.1 9.4 %copy-start.20 = (f32[8,768]{1,0:T(8,128)S(1)}, f32[8,768]{1,0:T(8,128)}, u32[]{:S(2)}) copy-start(f32[8,768]{1,0:T(8,128)} %get-tuple-element.146) | copy-start | bytes 73732
  396.1 9.4 %copy-start.22 = (f32[8,768]{1,0:T(8,128)S(1)}, f32[8,768]{1,0:T(8,128)}, u32[]{:S(2)}) copy-start(f32[8,768]{1,0:T(8,128)} %get-tuple-element.147) | copy-start | bytes 73732
  396.1 9.7 %copy-start.25 = (f32[1,3072]{1,0:T(1,128)S(1)}, f32[1,3072]{1,0:T(1,128)}, u32[]{:S(2)}) copy-start(f32[1,3072]{1,0:T(1,128)} %get-tuple-element.145) | copy-start | bytes 36868
  507.2 100.1 %collective-permute-start.10 = (bf16[256,768]{1,0:T(8,128)(2,1)S(1)}, bf16[256,768]{1,0:T(8,128)(2,1)S(1)}, u32[]{:S(2)}, u32[]{:S(2)}) collective-permute-start(bf16[256,768]{1,0:T(8,128)(2,1)S(1)} %get-tuple-element.165), channel_id=1, source_target_pairs={{0,2},{1,3},{2,0},{3,1},{4,6},{5,7},{6,4},{7,5},{8,10},{9,11},{10,... | collective-permute-start | bytes 1179656 | tf_op jit(solution)/shard_map/ppermute | solution.py:858
  602.4 5.9 copy-start.11
  602.5 6.6 %copy-start.9 = (f32[24,3072]{1,0:T(8,128)S(1)}, f32[24,3072]{1,0:T(8,128)}, u32[]{:S(2)}) copy-start(f32[24,3072]{1,0:T(8,128)} %get-tuple-element.253) | copy-start | bytes 884740
  602.5 7.3 %copy-start.8 = (f32[96,768]{1,0:T(8,128)S(1)}, f32[96,768]{1,0:T(8,128)}, u32[]{:S(2)}) copy-start(f32[96,768]{1,0:T(8,128)} %get-tuple-element.255) | copy-start | bytes 884740
  (34 other events, 135.9 us)
